TPU v7x, 32 devices: a whole 2x2x4 slice. The times are simulated.
32 devices in a mesh: row: 4 (over x, core), col: 8 (over z, y).
Axes of the slice: x: 2, y: 2, z: 4, core: 2. Of those that a mesh axis runs over, the one named last changes fastest.
Arguments:
- embeddings: bfloat16 [24576, 1024], P(('row', 'col')), may hold values from -40 to 40
- doc_ids: int32 [24576], P(('row', 'col')), may hold values from 0 to 24575, each once
- valid_counts: int32 [32], P(('row', 'col')), may hold values from 384 to 768
Outputs:
- nearest: float32 [24576], P(('row', 'col'))
Inputs may be any that keep to these rules, and one draw needn't show every extreme that they name: `doc_ids`: the ids are distinct.
All inputs are finite; a program needn't handle non-finite values.
Results may differ from a plain program's by a relative error of at most 0.0005.
Values may be sent and summed in bfloat16 or wider, within the bound.
No kernel may reach another device: no remote copies, remote signals or barrier semaphores. Data moves between devices by JAX's collectives and lax.ppermute only.
A program may use at most 64 MiB of HBM per device.

v0:
```python
import functools

import jax
import jax.numpy as jnp
from jax import lax
from jax.experimental import pallas as pl
from jax.experimental.pallas import tpu as pltpu
from jax.sharding import PartitionSpec as P


BAND = 4
Y = BAND // 2
HEAD = 16
TILE = 256
LANES = 128
AXES = ("row", "col")


class Plan:
    def __init__(self, rows, cols):
        self.R, self.Z, self.C = rows, cols // Y, cols
        Z, R = self.Z, self.R
        even, odd, gate = range(0, R, 2), range(1, R, 2), range(1, R - 1, 2)
        at, ys = self.at, range(Y)
        self.swap_odd = [(at(r, z, y), at(r, z, 1 - y)) for r in odd for z in range(Z) for y in ys]
        self.swap_even = [(at(r, z, y), at(r, z, 1 - y)) for r in even for z in range(Z) for y in ys]
        self.first = [(at(r, z, y), at(r, z - 1, y)) for r in even for z in range(1, Z) for y in ys]
        self.first += [(at(r, z, y), at(r, z + 1, y)) for r in odd for z in range(Z - 1) for y in ys]
        self.second = [(at(r, z, y), at(r, z - 1, y)) for r in even for z in range(1, Z - 1) for y in ys]
        self.second += [(at(r, z, y), at(r, z + 1, y)) for r in odd for z in range(1, Z - 1) for y in ys]
        self.side = [(at(r, 0, y), at(r, 1, y)) for r in odd for y in ys]
        self.side += [(at(r, Z - 1, y), at(r, Z - 2, y)) for r in gate for y in ys]
        self.kin = [(at(r, Z - 4, y), at(r + 1, 0, y)) for r in even for y in ys]
        self.kin += [(at(r, Z - 3, y), at(r + 1, 1, y)) for r in even for y in ys]
        self.across = [(at(r, Z - 1, y), at(r + 1, Z - 1, y)) for r in gate for y in ys]
        self.across += [(at(r + 1, 0, y), at(r, 0, y)) for r in gate for y in ys]
        self.top = [(at(r + 1, Z - 1, y), at(r, Z - 2, y)) for r in gate for y in ys]
        self.gate_a = [(at(r + 1, 0, y), at(r, Z - 2, y)) for r in gate for y in ys]
        self.gate_a += [(at(r, Z - 1, y), at(r + 1, 1, y)) for r in gate for y in ys]
        self.gate_b = [(at(r, 0, y), at(r, Z - 2, y)) for r in gate for y in ys]
        self.gate_b += [(at(r + 1, Z - 1, y), at(r + 1, 1, y)) for r in gate for y in ys]
        self.first_back = [(b, a) for a, b in self.first]
        self.second_back = [(at(r, z, y), at(r, z + 2, y)) for r in even for z in range(Z - 2) for y in ys]
        self.second_back += [(at(r, z, y), at(r, z - 2, y)) for r in odd for z in range(2, Z) for y in ys]
        self.kin_back = [(at(r + 1, 0, y), at(r, Z - 2, y)) for r in even for y in ys]
        self.kin_back += [(at(r + 1, 1, y), at(r, Z - 1, y)) for r in even for y in ys]
        self.side_back = [(at(r, 1, y), at(r, 0, 1 - y)) for r in odd for y in ys]
        self.side_back_late = [(at(r, Z - 2, y), at(r, Z - 1, 1 - y)) for r in gate for y in ys]
        self.top_back = [(at(r, Z - 2, y), at(r, Z - 1, y)) for r in gate for y in ys]
        self.gate_back = [(b, a) for a, b in self.gate_a]
        self.swap = self.swap_even + self.swap_odd
        self.swap_late = [(at(r, Z - 2, y), at(r, Z - 2, 1 - y)) for r in gate for y in ys]
        self.swap_late += [(at(r + 1, 1, y), at(r + 1, 1, 1 - y)) for r in gate for y in ys]

    def at(self, r, z, y):
        return r * self.C + z * Y + y

    def place(self, index):
        r, c = index // self.C, index % self.C
        return r, c // Y, c % Y


def permute(block, pairs):
    return lax.ppermute(block, AXES, pairs)


def pack_kernel(docs, count_ref, emb_ref, ids_ref, out_ref):
    n = emb_ref.shape[0]
    lane = lax.broadcasted_iota(jnp.int32, (1, n), 1)
    code = jnp.where(lane < count_ref[0], docs - ids_ref[...], 0)
    row = lax.broadcasted_iota(jnp.int32, (HEAD, n), 0)
    head = jnp.where(row == 0, code & 255, jnp.where(row == 1, (code >> 8) & 255, jnp.where(row == 2, code >> 16, 0)))
    out_ref[:HEAD, :n] = head.astype(jnp.float32).astype(jnp.bfloat16)
    if out_ref.shape[1] > n:
        out_ref[:HEAD, n:] = jnp.zeros((HEAD, out_ref.shape[1] - n), jnp.bfloat16)
    step = LANES

    def body(i, _):
        x = emb_ref[pl.ds(pl.multiple_of(i * step, step), step), :].astype(jnp.float32)
        total = jnp.sum(x * x, axis=-1, keepdims=True)
        out_ref[pl.ds(pl.multiple_of(HEAD + i * step, HEAD), step), :] = (x * lax.rsqrt(total + 1e-06)).astype(jnp.bfloat16)
        return 0

    lax.fori_loop(0, n // step, body, 0)


def codes(ref, n):
    head = ref[:HEAD, :n].astype(jnp.float32)
    return head[0:1] + 256.0 * head[1:2] + 65536.0 * head[2:3]


def spread(row, out_ref):
    for g in range(row.shape[1] // LANES):
        block = jnp.broadcast_to(row[:, g * LANES : (g + 1) * LANES], (LANES, LANES))
        out_ref[g * LANES : (g + 1) * LANES, :] = block.T


def gather_rows(acc_ref):
    parts = [
        jnp.max(acc_ref[g * LANES : (g + 1) * LANES, :].T, axis=0, keepdims=True)
        for g in range(acc_ref.shape[0] // LANES)
    ]
    return jnp.concatenate(parts, axis=1)


def pair_job(left_ref, spread_ref, right_ref, right_from, right_codes, row_acc, col_acc, scores_ref, col_from=0):
    n = spread_ref.shape[0]
    count = right_codes.shape[1]
    groups = range(0, count, LANES)

    def multiply(i):
        scores_ref[i % 2, :, :count] = lax.dot_general(
            left_ref[HEAD + i * TILE : HEAD + (i + 1) * TILE, :],
            right_ref[right_from : right_from + count, :],
            (((1,), (1,)), ((), ())),
            preferred_element_type=jnp.float32,
        )

    def reduce(i):
        ups = [None] * len(groups)
        theirs = [jnp.broadcast_to(right_codes[:, g : g + LANES], (8, LANES)) for g in groups]
        for j in range(i * TILE, (i + 1) * TILE, 8):
            mine = spread_ref[j : j + 8, :]
            best = row_acc[j : j + 8, :] if row_acc is not None else None
            for k, g in enumerate(groups):
                part = scores_ref[i % 2, j - i * TILE : j - i * TILE + 8, g : g + LANES]
                lower = theirs[k] > mine
                if row_acc is not None:
                    best = jnp.maximum(best, jnp.where(lower, part, -1.0))
                if col_acc is not None:
                    up = jnp.where(lower, -1.0, part)
                    ups[k] = up if ups[k] is None else jnp.maximum(ups[k], up)
            if row_acc is not None:
                row_acc[j : j + 8, :] = best
        if col_acc is not None:
            for k, g in enumerate(groups):
                spot = slice(col_from + g, col_from + g + LANES)
                col_acc[:, spot] = jnp.maximum(col_acc[:, spot], ups[k])

    last = n // TILE - 1
    multiply(0)
    for i in range(1, last + 1):
        multiply(i)
        reduce(i - 1)
    reduce(last)


def clear(*refs):
    for ref in refs:
        ref[...] = jnp.full(ref.shape, -1.0, jnp.float32)


def put_rows(out_ref, acc_ref, *so_far):
    found = gather_rows(acc_ref)
    for ref in so_far:
        found = jnp.maximum(found, ref[...])
    out_ref[...] = found


def put_cols(out_ref, acc_ref, *so_far):
    found = jnp.max(acc_ref[...], axis=0, keepdims=True)
    for ref in so_far:
        found = jnp.maximum(found, ref[...])
    out_ref[...] = found


class Fetch:
    def __init__(self, needed, source, target, sem):
        self.needed, self.target = needed, target
        self.copy = pltpu.make_async_copy(source, target, sem)

    def start(self):
        if self.needed is True:
            self.copy.start()
        else:
            pl.when(self.needed)(self.copy.start)

    def wait(self):
        if self.needed is True:
            self.copy.wait()
        else:
            pl.when(self.needed)(self.copy.wait)
        return self.target


def fetches(refs, held, sems, needed):
    out = [Fetch(c, ref, h, sems.at[i]) for i, (ref, h, c) in enumerate(zip(refs, held, needed))]
    for f in out:
        f.start()
    return out


def position(plan, index_ref):
    index = index_ref[0]
    r, c = index // plan.C, index % plan.C
    return r, c // Y, c % Y, r % 2 == 0


def self_kernel(plan, index_ref, own_hbm, own_out, own_v, sems, scores, own_codes, own_best):
    n = own_codes.shape[0]
    (own,) = fetches([own_hbm], [own_v], sems, [True])
    clear(own_best)
    own = own.wait()
    row = codes(own, n)
    spread(row, own_codes)
    pair_job(own, own_codes, own, HEAD, row, own_best, None, scores)
    put_rows(own_out, own_best)


def first_kernel(plan, index_ref, own_hbm, r1_hbm, odd_hbm, own_out, y_out, r1_out, own_v, r1_v, odd_v, sems, scores, own_codes, y_codes, own_best, y_best, r1_best):
    n = own_codes.shape[0]
    _, z, _, even = position(plan, index_ref)
    has_r1 = jnp.where(even, z <= plan.Z - 2, z >= 1)
    own, r1, odd = fetches([own_hbm, r1_hbm, odd_hbm], [own_v, r1_v, odd_v], sems, [True, has_r1, ~even])
    clear(own_best, y_best, r1_best)
    own = own.wait()
    spread(codes(own, n), own_codes)
    r1 = r1.wait()

    @pl.when(has_r1)
    def _():
        pair_job(own, own_codes, r1, HEAD, codes(r1, n), own_best, r1_best, scores)

    held = odd.wait()

    @pl.when(~even)
    def _():
        row = codes(held, n)
        pair_job(own, own_codes, held, HEAD, row, own_best, None, scores)
        spread(row, y_codes)

    @pl.when((~even) & has_r1)
    def _():
        pair_job(held, y_codes, r1, HEAD, codes(r1, n), y_best, r1_best, scores)

    put_rows(own_out, own_best)
    put_rows(y_out, y_best)
    put_cols(r1_out, r1_best)


def second_kernel(plan, index_ref, own_hbm, r2_hbm, even_hbm, r1_hbm, odd_hbm, y_in, r1_in, own_out, y_out, r1_out, r2_out, own_v, r2_v, y_v, r1_v, sems, scores, own_codes, y_codes, own_best, y_best, r1_best, r2_best):
    n = own_codes.shape[0]
    _, z, y, even = position(plan, index_ref)
    has_r1 = even & (z <= plan.Z - 2)
    has_r2 = jnp.where(even, z <= plan.Z - 3, z >= 2)
    late_y = (~even) & has_r2 & (y == 1)
    own, r2, lower, r1, upper = fetches(
        [own_hbm, r2_hbm, even_hbm, r1_hbm, odd_hbm], [own_v, r2_v, y_v, r1_v, y_v], sems, [True, has_r2, even, has_r1, late_y]
    )
    clear(own_best, y_best, r1_best, r2_best)
    own = own.wait()
    spread(codes(own, n), own_codes)
    r2 = r2.wait()

    @pl.when(has_r2)
    def _():
        pair_job(own, own_codes, r2, HEAD, codes(r2, n), own_best, r2_best, scores)

    held = lower.wait()
    upper.wait()

    @pl.when(even)
    def _():
        pair_job(own, own_codes, held, HEAD, codes(held, n), own_best, None, scores)

    @pl.when(even | late_y)
    def _():
        spread(codes(held, n), y_codes)

    @pl.when((even & has_r2 & (y == 0)) | late_y)
    def _():
        pair_job(held, y_codes, r2, HEAD, codes(r2, n), y_best, r2_best, scores)

    r1 = r1.wait()

    @pl.when(has_r1)
    def _():
        pair_job(held, y_codes, r1, HEAD, codes(r1, n), y_best, r1_best, scores)

    put_rows(own_out, own_best)
    put_rows(y_out, y_best, y_in)
    put_cols(r1_out, r1_best, r1_in)
    put_cols(r2_out, r2_best)


def kin_kernel(plan, index_ref, own_hbm, kin_hbm, r1_hbm, side_hbm, odd_hbm, y_in, r1_in, own_out, y_out, r1_out, side_out, kin_out, own_v, kin_v, r1_v, side_v, odd_v, sems, scores, left_codes, own_best, y_best, r1_best, side_best, kin_best):
    n = left_codes.shape[0]
    _, z, y, even = position(plan, index_ref)
    here = (~even) & (z <= 1)
    both = (~even) & (z == 1)
    cross = here & (y == 1)
    own, kin, r1, side, odd = fetches(
        [own_hbm, kin_hbm, r1_hbm, side_hbm, odd_hbm], [own_v, kin_v, r1_v, side_v, odd_v], sems, [here, here, both, both, cross]
    )
    clear(own_best, y_best, r1_best, side_best, kin_best)
    own, kin = own.wait(), kin.wait()

    def meet(left, best):
        spread(codes(left, n), left_codes)
        pair_job(left, left_codes, kin, HEAD, codes(kin, n), best, kin_best, scores)

    @pl.when(here)
    def _():
        meet(own, own_best)

    r1, side = r1.wait(), side.wait()

    @pl.when(both)
    def _():
        meet(r1, r1_best)
        meet(side, side_best)

    odd = odd.wait()

    @pl.when(cross)
    def _():
        meet(odd, y_best)

    put_rows(own_out, own_best)
    put_rows(y_out, y_best, y_in)
    put_rows(r1_out, r1_best, r1_in)
    put_rows(side_out, side_best)
    put_cols(kin_out, kin_best)


def gate_kernel(plan, index_ref, own_hbm, ua_hbm, ub_hbm, top_hbm, side_hbm, even_hbm, odd_hbm, own_out, y_out, top_out, side_out, u_out, own_v, ua_v, ub_v, top_v, side_v, y_v, sems, scores, left_codes, own_best, y_best, top_best, side_best, u_best):
    n = left_codes.shape[0]
    half = n // 2
    r, z, y, even = position(plan, index_ref)
    low = (~even) & (z == plan.Z - 2) & (r < plan.R - 1)
    high = even & (z == 1) & (r >= 2)
    here = low | high
    own, ua, ub, top, side, lower, upper = fetches(
        [own_hbm, ua_hbm, ub_hbm, top_hbm, side_hbm, even_hbm, odd_hbm],
        [own_v, ua_v, ub_v, top_v, side_v, y_v, y_v],
        sems,
        [here, here, here, low, low, high & (y == 1), low & (y == 0)],
    )
    clear(own_best, y_best, top_best, side_best, u_best)
    own, ua, ub = own.wait(), ua.wait(), ub.wait()

    def meet(left, best):
        row = codes(ua, n)
        spread(codes(left, n), left_codes)
        pair_job(left, left_codes, ua, HEAD, row[:, :half], best, u_best, scores, 0)
        pair_job(left, left_codes, ub, 0, row[:, half:], best, u_best, scores, half)

    @pl.when(here)
    def _():
        meet(own, own_best)

    top, side = top.wait(), side.wait()

    @pl.when(low)
    def _():
        meet(top, top_best)
        meet(side, side_best)

    held = lower.wait()
    upper.wait()

    @pl.when((high & (y == 1)) | (low & (y == 0)))
    def _():
        meet(held, y_best)

    put_rows(own_out, own_best)
    put_rows(y_out, y_best)
    put_rows(top_out, top_best)
    put_rows(side_out, side_best)
    put_cols(u_out, u_best)


def finish_kernel(plan, index_ref, count_ref, own_0, own_1, own_2, own_3, own_4, second, first, swap, side, kin, gate, top, side_late, swap_late, out_ref):
    r, z, _, even = position(plan, index_ref)
    Z, R = plan.Z, plan.R
    found = functools.reduce(jnp.maximum, [ref[...] for ref in (own_0, own_1, own_2, own_3, own_4, swap)])
    inner = (~even) & (r < R - 1)
    returns = (
        (second, jnp.where(even, z >= 2, z <= Z - 3)),
        (first, jnp.where(even, z >= 1, z <= Z - 2)),
        (side, (~even) & (z == 0)),
        (kin, even & (z >= Z - 2)),
        (gate, (even & (r >= 2) & (z == 0)) | (inner & (z == Z - 1))),
        (top, inner & (z == Z - 1)),
        (side_late, inner & (z == Z - 1)),
        (swap_late, (inner & (z == Z - 2)) | (even & (r >= 2) & (z == 1))),
    )
    for ref, mine in returns:
        found = jnp.maximum(found, jnp.where(mine, ref[...], -1.0))
    lane = lax.broadcasted_iota(jnp.int32, found.shape, 1)
    out_ref[...] = jnp.where(lane < count_ref[0], found, -1.0)


SMEM, VMEM, ANY = (pl.BlockSpec(memory_space=m) for m in (pltpu.SMEM, pltpu.VMEM, pl.ANY))


def stage(kernel, plan, index, blocks, vectors, n, outs, spreads, rows, cols, jobs, held=None):
    vector = jax.ShapeDtypeStruct((1, n), jnp.float32)
    width = blocks[0].shape[1]
    held = blocks if held is None else held
    scratch = [pltpu.VMEM(b.shape, b.dtype) for b in held] + [pltpu.SemaphoreType.DMA((len(blocks),)), pltpu.VMEM((2, TILE, n), jnp.float32)]
    scratch += [pltpu.VMEM((n, LANES), jnp.float32)] * (spreads + rows) + [pltpu.VMEM((8, n), jnp.float32)] * cols
    return pl.pallas_call(
        functools.partial(kernel, plan),
        out_shape=[vector] * outs,
        in_specs=[SMEM] + [ANY] * len(blocks) + [VMEM] * len(vectors),
        out_specs=[VMEM] * outs,
        scratch_shapes=scratch,
        cost_estimate=pl.CostEstimate(flops=2 * n * n * width * jobs, bytes_accessed=2 * n * width * len(blocks), transcendentals=0),
    )(index, *blocks, *vectors)


def local(plan, docs, embeddings, doc_ids, valid_counts):
    return body(plan, docs, embeddings, doc_ids, valid_counts)


def body(plan, docs, embeddings, doc_ids, valid_counts):
    n, width = embeddings.shape
    half = HEAD + n // 2
    at = (lax.axis_index("row") * plan.C + lax.axis_index("col")).astype(jnp.int32).reshape(1)
    own = pl.pallas_call(
        functools.partial(pack_kernel, docs),
        out_shape=jax.ShapeDtypeStruct((HEAD + n, width), jnp.bfloat16),
        in_specs=[SMEM, VMEM, VMEM],
        out_specs=VMEM,
        cost_estimate=pl.CostEstimate(flops=4 * n * width, bytes_accessed=4 * n * width, transcendentals=n),
        name="pack",
    )(valid_counts, embeddings, doc_ids.reshape(1, n))

    r1 = permute(own, plan.first)
    odd = permute(own, plan.swap_odd)
    moved = permute(own, plan.across)
    (own_0,) = stage(self_kernel, plan, at, [own], [], n, 1, 1, 1, 0, 1)
    own_a, moved_b = own[:half], moved[half:]
    r2 = permute(r1, plan.second)
    side = permute(odd, plan.side)
    top = permute(moved, plan.top)
    own_late, _ = lax.optimization_barrier((own, r1))
    even = permute(own_late, plan.swap_even)
    own_1, y_1, r1_1 = stage(first_kernel, plan, at, [own, r1, odd], [], n, 3, 2, 2, 1, 3)
    kin = permute(r2, plan.kin)
    own_a, moved_b, _ = lax.optimization_barrier((own_a, moved_b, r2))
    ua = permute(own_a, plan.gate_a)
    ub = permute(moved_b, plan.gate_b)
    own_2, y_2, r1_2, r2_2 = stage(second_kernel, plan, at, [own, r2, even, r1, odd], [y_1, r1_1], n, 4, 2, 2, 2, 4, held=[own, r2, even, r1])
    own_3, y_3, r1_3, side_3, kin_3 = stage(kin_kernel, plan, at, [own, kin, r1, side, odd], [y_2, r1_2], n, 5, 1, 4, 1, 4)
    own_4, y_4, top_4, side_4, u_4 = stage(gate_kernel, plan, at, [own, ua, ub, top, side, even, odd], [], n, 5, 1, 4, 1, 4, held=[own, ua, ub, top, side, even])

    returned = [
        permute(r2_2, plan.second_back),
        permute(r1_3, plan.first_back),
        permute(y_3, plan.swap),
        permute(side_3, plan.side_back),
        permute(kin_3, plan.kin_back),
        permute(u_4, plan.gate_back),
        permute(top_4, plan.top_back),
        permute(side_4, plan.side_back_late),
        permute(y_4, plan.swap_late),
    ]
    nearest = pl.pallas_call(
        functools.partial(finish_kernel, plan),
        out_shape=jax.ShapeDtypeStruct((1, n), jnp.float32),
        in_specs=[SMEM, SMEM] + [VMEM] * 14,
        out_specs=VMEM,
        name="finish",
    )(at, valid_counts, own_0, own_1, own_2, own_3, own_4, *returned)
    return nearest.reshape(n)


def solution(mesh):
    plan = Plan(mesh.shape["row"], mesh.shape["col"])

    def whole(embeddings, doc_ids, valid_counts):
        step = jax.shard_map(
            functools.partial(local, plan, doc_ids.shape[0]),
            mesh=mesh,
            in_specs=(P(AXES, None), P(AXES), P(AXES)),
            out_specs=P(AXES),
            check_vma=False,
        )
        return step(embeddings, doc_ids, valid_counts)

    return whole
```

profile of v0, /device:TPU:2, one launch (start us, length us, event | category | flops | bytes accessed | tf_op | source)
XLA Modules:
  0.0 100.2 jit_solution(17008729562601800143)
XLA Ops:
  0.7 1.3 %reshape.10.ids_ref = s32[1,768]{1,0:T(1,128)} reshape(s32[768]{0:T(1024)} %param.4) | data formatting | bytes 6144 | tf_op jit(solution)/shard_map/reshape | solution.py:428
  1.9 3.5 %pack.1.own_hbm = bf16[784,1024]{1,0:T(8,128)(2,1)} custom-call(s32[1]{0:T(128)S(6)} %copy.4.count_ref, bf16[768,1024]{1,0:T(8,128)(2,1)} %emb_ref.1, s32[1,768]{1,0:T(1,128)} %reshape.10.ids_ref), custom_call_target="tpu_custom_call" | custom-call | flops 3145728 | bytes 3145728 | tf_op jit(solution)/shard_map/pack/pallas_call | solution.py:421
  5.4 1.3 %collective-permute-start = (bf16[784,1024]{1,0:T(8,128)(2,1)}, bf16[784,1024]{1,0:T(8,128)(2,1)S(1)}, u32[]{:S(2)}, u32[]{:S(2)}) collective-permute-start(bf16[784,1024]{1,0:T(8,128)(2,1)} %pack.1.own_hbm), channel_id=1, source_target_pairs={{2,0},{3,1},{4,2},{5,3},{6,4},{7,5},{18,16},{19,17},{20,18},{21,19... | collective-permute-start | bytes 4816904 | tf_op jit(solution)/shard_map/ppermute | solution.py:64
  6.7 1.8 %collective-permute-start.1 = (bf16[784,1024]{1,0:T(8,128)(2,1)}, bf16[784,1024]{1,0:T(8,128)(2,1)}, u32[]{:S(2)}, u32[]{:S(2)}) collective-permute-start(bf16[784,1024]{1,0:T(8,128)(2,1)} %pack.1.own_hbm), channel_id=1, source_target_pairs={{8,9},{9,8},{10,11},{11,10},{12,13},{13,12},{14,15},{15,14},{24,25... | collective-permute-start | bytes 4816904 | tf_op jit(solution)/shard_map/ppermute | solution.py:64
  8.5 5.3 %collective-permute-start.6 = (bf16[784,1024]{1,0:T(8,128)(2,1)}, bf16[784,1024]{1,0:T(8,128)(2,1)S(1)}, u32[]{:S(2)}, u32[]{:S(2)}) collective-permute-start(bf16[784,1024]{1,0:T(8,128)(2,1)} %pack.1.own_hbm), channel_id=1, source_target_pairs={{14,22},{15,23},{16,8},{17,9}} | collective-permute-start | bytes 4816904 | tf_op jit(solution)/shard_map/ppermute | solution.py:64
  13.8 14.4 %collective-permute-done.r1_hbm = bf16[784,1024]{1,0:T(8,128)(2,1)S(1)} collective-permute-done((bf16[784,1024]{1,0:T(8,128)(2,1)}, bf16[784,1024]{1,0:T(8,128)(2,1)S(1)}, u32[]{:S(2)}, u32[]{:S(2)}) %collective-permute-start) | collective-permute-done | bytes 1605664 | tf_op jit(solution)/shard_map/ppermute | solution.py:64
  28.2 1.3 %collective-permute-start.2 = (bf16[784,1024]{1,0:T(8,128)(2,1)S(1)}, bf16[784,1024]{1,0:T(8,128)(2,1)}, u32[]{:S(2)}, u32[]{:S(2)}) collective-permute-start(bf16[784,1024]{1,0:T(8,128)(2,1)S(1)} %collective-permute-done.r1_hbm), channel_id=1, source_target_pairs={{2,0},{3,1},{4,2},{5,3},{18,16},{19,17},{20,18},{21,19},{10,12},{1... | collective-permute-start | bytes 4816904 | tf_op jit(solution)/shard_map/ppermute | solution.py:64
  29.5 3.4 %collective-permute-start.3 = (bf16[784,1024]{1,0:T(8,128)(2,1)}, bf16[784,1024]{1,0:T(8,128)(2,1)}, u32[]{:S(2)}, u32[]{:S(2)}) collective-permute-start(bf16[784,1024]{1,0:T(8,128)(2,1)} %pack.1.own_hbm), channel_id=1, source_target_pairs={{0,1},{1,0},{2,3},{3,2},{4,5},{5,4},{6,7},{7,6},{16,17},{17,16},{1... | collective-permute-start | bytes 4816904 | tf_op jit(solution)/shard_map/ppermute | solution.py:64
  33.0 0.0 collective-permute-done.1.odd_hbm
  33.0 1.9 %collective-permute-start.5 = (bf16[784,1024]{1,0:T(8,128)(2,1)}, bf16[784,1024]{1,0:T(8,128)(2,1)}, u32[]{:S(2)}, u32[]{:S(2)}) collective-permute-start(bf16[784,1024]{1,0:T(8,128)(2,1)} %collective-permute-done.1.odd_hbm), channel_id=1, source_target_pairs={{8,10},{9,11},{24,26},{25,27},{14,12},{15,13}} | collective-permute-start | bytes 4816904 | tf_op jit(solution)/shard_map/ppermute | solution.py:64
  34.9 0.0 collective-permute-done.6
  34.9 1.9 %collective-permute-start.9 = (bf16[784,1024]{1,0:T(8,128)(2,1)S(1)}, bf16[784,1024]{1,0:T(8,128)(2,1)}, u32[]{:S(2)}, u32[]{:S(2)}) collective-permute-start(bf16[784,1024]{1,0:T(8,128)(2,1)S(1)} %collective-permute-done.6), channel_id=1, source_target_pairs={{22,12},{23,13}} | collective-permute-start | bytes 4816904 | tf_op jit(solution)/shard_map/ppermute | solution.py:64
  36.8 14.2 %collective-permute-done.2.r2_hbm = bf16[784,1024]{1,0:T(8,128)(2,1)} collective-permute-done((bf16[784,1024]{1,0:T(8,128)(2,1)S(1)}, bf16[784,1024]{1,0:T(8,128)(2,1)}, u32[]{:S(2)}, u32[]{:S(2)}) %collective-permute-start.2) | collective-permute-done | bytes 1605664 | tf_op jit(solution)/shard_map/ppermute | solution.py:64
  51.0 2.5 %collective-permute-start.4 = (bf16[784,1024]{1,0:T(8,128)(2,1)}, bf16[784,1024]{1,0:T(8,128)(2,1)}, u32[]{:S(2)}, u32[]{:S(2)}) collective-permute-start(bf16[784,1024]{1,0:T(8,128)(2,1)} %collective-permute-done.2.r2_hbm), channel_id=1, source_target_pairs={{0,8},{1,9},{16,24},{17,25},{2,10},{3,11},{18,26},{19,27}} | collective-permute-start | bytes 4816904 | tf_op jit(solution)/shard_map/ppermute | solution.py:64
  53.5 1.2 %slice.8 = bf16[400,1024]{1,0:T(8,128)(2,1)S(1)} slice(bf16[784,1024]{1,0:T(8,128)(2,1)} %pack.1.own_hbm), slice={[0:400], [0:1024]} | slice | bytes 1638400 | tf_op jit(solution)/shard_map/slice | solution.py:434
  54.7 0.1 slice.9
  54.7 2.5 %collective-permute-start.7 = (bf16[400,1024]{1,0:T(8,128)(2,1)S(1)}, bf16[400,1024]{1,0:T(8,128)(2,1)}, u32[]{:S(2)}, u32[]{:S(2)}) collective-permute-start(bf16[400,1024]{1,0:T(8,128)(2,1)S(1)} %slice.8), channel_id=1, source_target_pairs={{16,12},{17,13},{14,18},{15,19}} | collective-permute-start | bytes 2457608 | tf_op jit(solution)/shard_map/ppermute | solution.py:64
  57.2 0.0 collective-permute-done.3.even_hbm
  57.2 1.5 %collective-permute-start.8 = (bf16[384,1024]{1,0:T(8,128)(2,1)S(1)}, bf16[384,1024]{1,0:T(8,128)(2,1)}, u32[]{:S(2)}, u32[]{:S(2)}) collective-permute-start(bf16[384,1024]{1,0:T(8,128)(2,1)S(1)} %slice.9), channel_id=1, source_target_pairs={{8,12},{9,13},{22,18},{23,19}} | collective-permute-start | bytes 2359304 | tf_op jit(solution)/shard_map/ppermute | solution.py:64
  58.7 4.3 %shard_map.38 = (f32[1,768]{1,0:T(1,128)}, f32[1,768]{1,0:T(1,128)}, f32[1,768]{1,0:T(1,128)}) custom-call(s32[1]{0:T(128)} %bitcast.index_ref, bf16[784,1024]{1,0:T(8,128)(2,1)} %pack.1.own_hbm, bf16[784,1024]{1,0:T(8,128)(2,1)} %copy-done.9, bf16[784,1024]{1,0:T(8,128)(2,1)} %collective-permute-done.1.odd_hbm), custom_call_target="tpu_custom_call" | custom-call | flops 3623878656 | bytes 4718592 | tf_op jit(solution)/shard_map/pallas_call | solution.py:403
  63.1 9.7 %shard_map.39 = (f32[1,768]{1,0:T(1,128)}, f32[1,768]{1,0:T(1,128)}, f32[1,768]{1,0:T(1,128)}, f32[1,768]{1,0:T(1,128)}) custom-call(s32[1]{0:T(128)} %bitcast.index_ref, bf16[784,1024]{1,0:T(8,128)(2,1)} %pack.1.own_hbm, bf16[784,1024]{1,0:T(8,128)(2,1)} %collective-permute-done.2.r2_hbm, bf16[784,1024]{1,0:T(8,128)(2,1)} %collective-permute-done.3.even_hbm, ...), custom_call_target="tpu_custom_call" | custom-call | flops 4831838208 | bytes 7864320 | tf_op jit(solution)/shard_map/pallas_call | solution.py:403
  72.7 0.0 collective-permute-done.5.side_hbm
  72.7 1.3 %collective-permute-start.10 = (f32[1,768]{1,0:T(1,128)}, f32[1,768]{1,0:T(1,128)S(1)}, u32[]{:S(2)}, u32[]{:S(2)}) collective-permute-start(f32[1,768]{1,0:T(1,128)} %get-tuple-element.36), channel_id=1, source_target_pairs={{0,4},{1,5},{2,6},{3,7},{16,20},{17,21},{18,22},{19,23},{12,8},{13... | collective-permute-start | bytes 9224 | tf_op jit(solution)/shard_map/ppermute | solution.py:64
  74.0 0.0 collective-permute-done.9.top_hbm
  74.1 0.0 collective-permute-done.8.ub_hbm
  74.1 0.0 collective-permute-done.7.ua_hbm
  74.1 1.4 %shard_map.41 = (f32[1,768]{1,0:T(1,128)}, f32[1,768]{1,0:T(1,128)}, f32[1,768]{1,0:T(1,128)}, f32[1,768]{1,0:T(1,128)}, f32[1,768]{1,0:T(1,128)}) custom-call(s32[1]{0:T(128)} %bitcast.index_ref, bf16[784,1024]{1,0:T(8,128)(2,1)} %pack.1.own_hbm, bf16[400,1024]{1,0:T(8,128)(2,1)} %collective-permute-done.7.ua_hbm, ...), custom_call_target="tpu_custom_call" | custom-call | flops 4831838208 | bytes 11010048 | tf_op jit(solution)/shard_map/pallas_call | solution.py:403
  75.5 1.3 %collective-permute-start.15 = (f32[1,768]{1,0:T(1,128)}, f32[1,768]{1,0:T(1,128)S(1)}, u32[]{:S(2)}, u32[]{:S(2)}) collective-permute-start(f32[1,768]{1,0:T(1,128)} %get-tuple-element.41), channel_id=1, source_target_pairs={{12,16},{13,17},{18,14},{19,15}} | collective-permute-start | bytes 9224 | tf_op jit(solution)/shard_map/ppermute | solution.py:64
  76.8 0.7 collective-permute-start.16
  77.5 0.7 collective-permute-start.17
  78.2 0.0 collective-permute-done.4.kin_hbm
  78.2 0.7 collective-permute-start.18
  78.9 2.1 %shard_map.40 = (f32[1,768]{1,0:T(1,128)}, f32[1,768]{1,0:T(1,128)}, f32[1,768]{1,0:T(1,128)}, f32[1,768]{1,0:T(1,128)}, f32[1,768]{1,0:T(1,128)}) custom-call(s32[1]{0:T(128)} %bitcast.index_ref, bf16[784,1024]{1,0:T(8,128)(2,1)} %pack.1.own_hbm, bf16[784,1024]{1,0:T(8,128)(2,1)} %collective-permute-done.4.kin_hbm, bf16[784,1024]{1,0:T(8,128)(2,1)} %copy-done.9, ...), custom_call_target="tpu_custom_call" | custom-call | flops 4831838208 | bytes 7864320 | tf_op jit(solution)/shard_map/pallas_call | solution.py:403
  81.0 0.0 collective-permute-done.10.second
  81.0 10.8 %collective-permute-start.11 = (f32[1,768]{1,0:T(1,128)}, f32[1,768]{1,0:T(1,128)S(1)}, u32[]{:S(2)}, u32[]{:S(2)}) collective-permute-start(f32[1,768]{1,0:T(1,128)} %get-tuple-element.37), channel_id=1, source_target_pairs={{0,2},{1,3},{2,4},{3,5},{4,6},{5,7},{16,18},{17,19},{18,20},{19,21... | collective-permute-start | bytes 9224 | tf_op jit(solution)/shard_map/ppermute | solution.py:64
  91.8 0.1 collective-permute-start.12
  91.9 0.7 collective-permute-start.13
  92.6 0.7 collective-permute-start.14
  93.3 3.5 %shard_map.37.own_0 = f32[1,768]{1,0:T(1,128)} custom-call(s32[1]{0:T(128)} %bitcast.index_ref, bf16[784,1024]{1,0:T(8,128)(2,1)} %pack.1.own_hbm), custom_call_target="tpu_custom_call" | custom-call | flops 1207959552 | bytes 1572864 | tf_op jit(solution)/shard_map/pallas_call | solution.py:403
  96.8 0.0 collective-permute-done.18.swap_late
  96.9 0.0 collective-permute-done.13.side
  96.9 0.5 copy-done.4
  97.4 0.0 copy-done.5
  97.4 0.0 copy-done.6
  97.5 0.0 copy-done.7
  97.5 0.0 copy-done.8
  97.5 1.4 %finish.1 = f32[1,768]{1,0:T(1,128)} custom-call(s32[1]{0:T(128)} %bitcast.index_ref, s32[1]{0:T(128)S(6)} %copy.4.count_ref, f32[1,768]{1,0:T(1,128)} %shard_map.37.own_0, f32[1,768]{1,0:T(1,128)} %get-tuple-element.25.own_1, f32[1,768]{1,0:T(1,128)} %get-tuple-element.29.own_2, f32[1,768]{1,0:T(1,128)} %get-tuple-element.32.own_3, ...), custom_call_target="tpu_custom_call" | custom-call | tf_op jit(solution)/shard_map/finish/pallas_call | solution.py:460
  98.9 1.3 %reduce = f32[768]{0:T(1024)} reduce(f32[1,768]{1,0:T(1,128)} %finish.1, f32[]{:T(128)} %constant.11), dimensions={0}, to_apply=%pallas_call.61.reduce_sub_computation | reduce | bytes 6148 | tf_op jit(solution)/shard_map/finish/pallas_call | solution.py:460
  (21 shorter events, 0.0 us)
Async XLA Ops:
  5.4 22.9 %collective-permute-start = (bf16[784,1024]{1,0:T(8,128)(2,1)}, bf16[784,1024]{1,0:T(8,128)(2,1)S(1)}, u32[]{:S(2)}, u32[]{:S(2)}) collective-permute-start(bf16[784,1024]{1,0:T(8,128)(2,1)} %pack.1.own_hbm), channel_id=1, source_target_pairs={{2,0},{3,1},{4,2},{5,3},{6,4},{7,5},{18,16},{19,17},{20,18},{21,19... | collective-permute-start | bytes 4816904 | tf_op jit(solution)/shard_map/ppermute | solution.py:64
  6.7 26.3 %collective-permute-start.1 = (bf16[784,1024]{1,0:T(8,128)(2,1)}, bf16[784,1024]{1,0:T(8,128)(2,1)}, u32[]{:S(2)}, u32[]{:S(2)}) collective-permute-start(bf16[784,1024]{1,0:T(8,128)(2,1)} %pack.1.own_hbm), channel_id=1, source_target_pairs={{8,9},{9,8},{10,11},{11,10},{12,13},{13,12},{14,15},{15,14},{24,25... | collective-permute-start | bytes 4816904 | tf_op jit(solution)/shard_map/ppermute | solution.py:64
  8.5 26.4 %collective-permute-start.6 = (bf16[784,1024]{1,0:T(8,128)(2,1)}, bf16[784,1024]{1,0:T(8,128)(2,1)S(1)}, u32[]{:S(2)}, u32[]{:S(2)}) collective-permute-start(bf16[784,1024]{1,0:T(8,128)(2,1)} %pack.1.own_hbm), channel_id=1, source_target_pairs={{14,22},{15,23},{16,8},{17,9}} | collective-permute-start | bytes 4816904 | tf_op jit(solution)/shard_map/ppermute | solution.py:64
  28.2 22.8 %copy-start.9 = (bf16[784,1024]{1,0:T(8,128)(2,1)}, bf16[784,1024]{1,0:T(8,128)(2,1)S(1)}, u32[]{:S(2)}) copy-start(bf16[784,1024]{1,0:T(8,128)(2,1)S(1)} %collective-permute-done.r1_hbm) | copy-start | bytes 4816900
  28.2 22.8 %collective-permute-start.2 = (bf16[784,1024]{1,0:T(8,128)(2,1)S(1)}, bf16[784,1024]{1,0:T(8,128)(2,1)}, u32[]{:S(2)}, u32[]{:S(2)}) collective-permute-start(bf16[784,1024]{1,0:T(8,128)(2,1)S(1)} %collective-permute-done.r1_hbm), channel_id=1, source_target_pairs={{2,0},{3,1},{4,2},{5,3},{18,16},{19,17},{20,18},{21,19},{10,12},{1... | collective-permute-start | bytes 4816904 | tf_op jit(solution)/shard_map/ppermute | solution.py:64
  29.5 27.7 %collective-permute-start.3 = (bf16[784,1024]{1,0:T(8,128)(2,1)}, bf16[784,1024]{1,0:T(8,128)(2,1)}, u32[]{:S(2)}, u32[]{:S(2)}) collective-permute-start(bf16[784,1024]{1,0:T(8,128)(2,1)} %pack.1.own_hbm), channel_id=1, source_target_pairs={{0,1},{1,0},{2,3},{3,2},{4,5},{5,4},{6,7},{7,6},{16,17},{17,16},{1... | collective-permute-start | bytes 4816904 | tf_op jit(solution)/shard_map/ppermute | solution.py:64
  33.0 39.8 %collective-permute-start.5 = (bf16[784,1024]{1,0:T(8,128)(2,1)}, bf16[784,1024]{1,0:T(8,128)(2,1)}, u32[]{:S(2)}, u32[]{:S(2)}) collective-permute-start(bf16[784,1024]{1,0:T(8,128)(2,1)} %collective-permute-done.1.odd_hbm), channel_id=1, source_target_pairs={{8,10},{9,11},{24,26},{25,27},{14,12},{15,13}} | collective-permute-start | bytes 4816904 | tf_op jit(solution)/shard_map/ppermute | solution.py:64
  34.9 39.2 %collective-permute-start.9 = (bf16[784,1024]{1,0:T(8,128)(2,1)S(1)}, bf16[784,1024]{1,0:T(8,128)(2,1)}, u32[]{:S(2)}, u32[]{:S(2)}) collective-permute-start(bf16[784,1024]{1,0:T(8,128)(2,1)S(1)} %collective-permute-done.6), channel_id=1, source_target_pairs={{22,12},{23,13}} | collective-permute-start | bytes 4816904 | tf_op jit(solution)/shard_map/ppermute | solution.py:64
  51.0 27.2 %collective-permute-start.4 = (bf16[784,1024]{1,0:T(8,128)(2,1)}, bf16[784,1024]{1,0:T(8,128)(2,1)}, u32[]{:S(2)}, u32[]{:S(2)}) collective-permute-start(bf16[784,1024]{1,0:T(8,128)(2,1)} %collective-permute-done.2.r2_hbm), channel_id=1, source_target_pairs={{0,8},{1,9},{16,24},{17,25},{2,10},{3,11},{18,26},{19,27}} | collective-permute-start | bytes 4816904 | tf_op jit(solution)/shard_map/ppermute | solution.py:64
  54.7 19.3 %collective-permute-start.7 = (bf16[400,1024]{1,0:T(8,128)(2,1)S(1)}, bf16[400,1024]{1,0:T(8,128)(2,1)}, u32[]{:S(2)}, u32[]{:S(2)}) collective-permute-start(bf16[400,1024]{1,0:T(8,128)(2,1)S(1)} %slice.8), channel_id=1, source_target_pairs={{16,12},{17,13},{14,18},{15,19}} | collective-permute-start | bytes 2457608 | tf_op jit(solution)/shard_map/ppermute | solution.py:64
  57.2 16.9 %collective-permute-start.8 = (bf16[384,1024]{1,0:T(8,128)(2,1)S(1)}, bf16[384,1024]{1,0:T(8,128)(2,1)}, u32[]{:S(2)}, u32[]{:S(2)}) collective-permute-start(bf16[384,1024]{1,0:T(8,128)(2,1)S(1)} %slice.9), channel_id=1, source_target_pairs={{8,12},{9,13},{22,18},{23,19}} | collective-permute-start | bytes 2359304 | tf_op jit(solution)/shard_map/ppermute | solution.py:64
  72.7 8.2 %collective-permute-start.10 = (f32[1,768]{1,0:T(1,128)}, f32[1,768]{1,0:T(1,128)S(1)}, u32[]{:S(2)}, u32[]{:S(2)}) collective-permute-start(f32[1,768]{1,0:T(1,128)} %get-tuple-element.36), channel_id=1, source_target_pairs={{0,4},{1,5},{2,6},{3,7},{16,20},{17,21},{18,22},{19,23},{12,8},{13... | collective-permute-start | bytes 9224 | tf_op jit(solution)/shard_map/ppermute | solution.py:64
  75.5 16.2 %collective-permute-start.15 = (f32[1,768]{1,0:T(1,128)}, f32[1,768]{1,0:T(1,128)S(1)}, u32[]{:S(2)}, u32[]{:S(2)}) collective-permute-start(f32[1,768]{1,0:T(1,128)} %get-tuple-element.41), channel_id=1, source_target_pairs={{12,16},{13,17},{18,14},{19,15}} | collective-permute-start | bytes 9224 | tf_op jit(solution)/shard_map/ppermute | solution.py:64
  76.8 15.0 %collective-permute-start.16 = (f32[1,768]{1,0:T(1,128)}, f32[1,768]{1,0:T(1,128)S(1)}, u32[]{:S(2)}, u32[]{:S(2)}) collective-permute-start(f32[1,768]{1,0:T(1,128)} %get-tuple-element.42), channel_id=1, source_target_pairs={{12,14},{13,15}} | collective-permute-start | bytes 9224 | tf_op jit(solution)/shard_map/ppermute | solution.py:64
  77.5 15.1 %collective-permute-start.17 = (f32[1,768]{1,0:T(1,128)}, f32[1,768]{1,0:T(1,128)S(1)}, u32[]{:S(2)}, u32[]{:S(2)}) collective-permute-start(f32[1,768]{1,0:T(1,128)} %get-tuple-element.43), channel_id=1, source_target_pairs={{12,15},{13,14}} | collective-permute-start | bytes 9224 | tf_op jit(solution)/shard_map/ppermute | solution.py:64
  78.2 18.6 %collective-permute-start.18 = (f32[1,768]{1,0:T(1,128)}, f32[1,768]{1,0:T(1,128)S(1)}, u32[]{:S(2)}, u32[]{:S(2)}) collective-permute-start(f32[1,768]{1,0:T(1,128)} %get-tuple-element.44), channel_id=1, source_target_pairs={{12,13},{13,12},{18,19},{19,18}} | collective-permute-start | bytes 9224 | tf_op jit(solution)/shard_map/ppermute | solution.py:64
  81.0 15.8 %copy-start = (f32[1,768]{1,0:T(1,128)}, f32[1,768]{1,0:T(1,128)S(1)}, u32[]{:S(2)}) copy-start(f32[1,768]{1,0:T(1,128)S(1)} %collective-permute-done.10.second) | copy-start | bytes 9220
  81.0 15.8 %collective-permute-start.11 = (f32[1,768]{1,0:T(1,128)}, f32[1,768]{1,0:T(1,128)S(1)}, u32[]{:S(2)}, u32[]{:S(2)}) collective-permute-start(f32[1,768]{1,0:T(1,128)} %get-tuple-element.37), channel_id=1, source_target_pairs={{0,2},{1,3},{2,4},{3,5},{4,6},{5,7},{16,18},{17,19},{18,20},{19,21... | collective-permute-start | bytes 9224 | tf_op jit(solution)/shard_map/ppermute | solution.py:64
  91.8 5.0 %copy-start.1 = (f32[1,768]{1,0:T(1,128)}, f32[1,768]{1,0:T(1,128)S(1)}, u32[]{:S(2)}) copy-start(f32[1,768]{1,0:T(1,128)S(1)} %collective-permute-done.15.gate) | copy-start | bytes 9220
  91.8 5.1 %collective-permute-start.12 = (f32[1,768]{1,0:T(1,128)}, f32[1,768]{1,0:T(1,128)S(1)}, u32[]{:S(2)}, u32[]{:S(2)}) collective-permute-start(f32[1,768]{1,0:T(1,128)} %get-tuple-element.38), channel_id=1, source_target_pairs={{0,1},{1,0},{2,3},{3,2},{4,5},{5,4},{6,7},{7,6},{16,17},{17,16},{1... | collective-permute-start | bytes 9224 | tf_op jit(solution)/shard_map/ppermute | solution.py:64
  91.9 4.9 %copy-start.2 = (f32[1,768]{1,0:T(1,128)}, f32[1,768]{1,0:T(1,128)S(1)}, u32[]{:S(2)}) copy-start(f32[1,768]{1,0:T(1,128)S(1)} %collective-permute-done.16.top) | copy-start | bytes 9220
  91.9 5.0 %collective-permute-start.13 = (f32[1,768]{1,0:T(1,128)}, f32[1,768]{1,0:T(1,128)S(1)}, u32[]{:S(2)}, u32[]{:S(2)}) collective-permute-start(f32[1,768]{1,0:T(1,128)} %get-tuple-element.39), channel_id=1, source_target_pairs={{10,9},{11,8},{26,25},{27,24}} | collective-permute-start | bytes 9224 | tf_op jit(solution)/shard_map/ppermute | solution.py:64
  92.6 4.2 %copy-start.3 = (f32[1,768]{1,0:T(1,128)}, f32[1,768]{1,0:T(1,128)S(1)}, u32[]{:S(2)}) copy-start(f32[1,768]{1,0:T(1,128)S(1)} %collective-permute-done.17.side_late) | copy-start | bytes 9220
  92.6 4.3 %collective-permute-start.14 = (f32[1,768]{1,0:T(1,128)}, f32[1,768]{1,0:T(1,128)S(1)}, u32[]{:S(2)}, u32[]{:S(2)}) collective-permute-start(f32[1,768]{1,0:T(1,128)} %get-tuple-element.40), channel_id=1, source_target_pairs={{8,4},{9,5},{24,20},{25,21},{10,6},{11,7},{26,22},{27,23}} | collective-permute-start | bytes 9224 | tf_op jit(solution)/shard_map/ppermute | solution.py:64
  96.8 0.6 copy-start.4
  96.8 0.6 copy-start.5
  96.9 0.6 copy-start.6
  96.9 0.6 copy-start.7
  96.9 0.6 copy-start.8
where the time goes:
time: 101 us; the launch traced here: 100 us
  starting transfers between devices  40.1 us (40%)
  waiting for transfers between devices  28.7 us (28%)
  Pallas kernels  25.9 us (26%)
  local copies, waits for them, and re-layouts  3.13 us (3%)
  other arithmetic  1.28 us (1%)
  between operations  1.03 us (1%)
    ppermute x19, starting transfers between devices, permute(): return lax.ppermute(block, AXES, pairs)  40.1 us
    ppermute x19, waiting for transfers between devices, permute(): return lax.ppermute(block, AXES, pairs)  28.7 us
    pallas_call x5, Pallas kernels, stage(): pl.pallas_call(functools.partial(kernel, plan), out_shape=[vector] * outs...  21.1 us
    pallas_call x1, Pallas kernels, body(): pl.pallas_call(functools.partial(pack_kernel, docs), out_shape=jax.ShapeD...  3.46 us
  transfers between devices with their start and end apart: 19, of which 2 were waited for; matrix products, arithmetic and copies ran while one was open for 1% of the time, Pallas kernels for 21%

commit v1 on v0

--- a/solution.py
+++ b/solution.py
@@ -1,4 +1,5 @@
 import functools
+import math
 
 import jax
 import jax.numpy as jnp
@@ -11,8 +12,10 @@
 BAND = 4
 Y = BAND // 2
 HEAD = 16
-TILE = 256
+TILE = 384
 LANES = 128
+PARTS = 6
+SPARE = 4 << 20
 AXES = ("row", "col")
 
 
@@ -64,24 +67,44 @@
     return lax.ppermute(block, AXES, pairs)
 
 
-def pack_kernel(docs, count_ref, emb_ref, ids_ref, out_ref):
-    n = emb_ref.shape[0]
+def pack_kernel(docs, count_ref, emb_hbm, ids_ref, out_hbm, emb, out, in_sems, out_sems):
+    n, width = emb_hbm.shape
+    steps = in_sems.shape[0]
+    size = n // steps
+
+    def taken(i):
+        rows = pl.ds(i * size, size)
+        return pltpu.make_async_copy(emb_hbm.at[rows], emb.at[rows], in_sems.at[i])
+
+    def given(i):
+        rows = pl.ds(HEAD + i * size, size) if i < steps else pl.ds(0, HEAD)
+        return pltpu.make_async_copy(out.at[rows], out_hbm.at[rows], out_sems.at[i])
+
+    for i in range(steps):
+        taken(i).start()
     lane = lax.broadcasted_iota(jnp.int32, (1, n), 1)
-    code = jnp.where(lane < count_ref[0], docs - ids_ref[...], 0)
+    code = jnp.where(lane < count_ref[0], docs - ids_ref[...].reshape(1, n), 0)
     row = lax.broadcasted_iota(jnp.int32, (HEAD, n), 0)
     head = jnp.where(row == 0, code & 255, jnp.where(row == 1, (code >> 8) & 255, jnp.where(row == 2, code >> 16, 0)))
-    out_ref[:HEAD, :n] = head.astype(jnp.float32).astype(jnp.bfloat16)
-    if out_ref.shape[1] > n:
-        out_ref[:HEAD, n:] = jnp.zeros((HEAD, out_ref.shape[1] - n), jnp.bfloat16)
-    step = LANES
-
-    def body(i, _):
-        x = emb_ref[pl.ds(pl.multiple_of(i * step, step), step), :].astype(jnp.float32)
-        total = jnp.sum(x * x, axis=-1, keepdims=True)
-        out_ref[pl.ds(pl.multiple_of(HEAD + i * step, HEAD), step), :] = (x * lax.rsqrt(total + 1e-06)).astype(jnp.bfloat16)
-        return 0
-
-    lax.fori_loop(0, n // step, body, 0)
+    out[:HEAD, :n] = head.astype(jnp.float32).astype(jnp.bfloat16)
+    if width > n:
+        out[:HEAD, n:] = jnp.zeros((HEAD, width - n), jnp.bfloat16)
+    given(steps).start()
+    part = 32
+    for i in range(steps):
+        taken(i).wait()
+
+        def scale(j, _):
+            at = i * size + j * part
+            x = emb[pl.ds(pl.multiple_of(at, HEAD), part), :].astype(jnp.float32)
+            total = jnp.sum(x * x, axis=-1, keepdims=True)
+            out[pl.ds(pl.multiple_of(HEAD + at, HEAD), part), :] = (x * lax.rsqrt(total + 1e-06)).astype(jnp.bfloat16)
+            return 0
+
+        lax.fori_loop(0, size // part, scale, 0, unroll=True)
+        given(i).start()
+    for i in range(steps + 1):
+        given(i).wait()
 
 
 def codes(ref, n):
@@ -103,15 +126,16 @@
     return jnp.concatenate(parts, axis=1)
 
 
-def pair_job(left_ref, spread_ref, right_ref, right_from, right_codes, row_acc, col_acc, scores_ref, col_from=0):
-    n = spread_ref.shape[0]
-    count = right_codes.shape[1]
-    groups = range(0, count, LANES)
+def pair_job(left_ref, left_from, spread_ref, right_ref, right_codes, row_acc, col_acc, scores_ref, rows=None):
+    start, stop = rows or (0, spread_ref.shape[0])
+    n = right_codes.shape[1]
+    groups = range(0, n, LANES)
+    tiles = range((stop - start) // TILE)
 
     def multiply(i):
-        scores_ref[i % 2, :, :count] = lax.dot_general(
-            left_ref[HEAD + i * TILE : HEAD + (i + 1) * TILE, :],
-            right_ref[right_from : right_from + count, :],
+        scores_ref[i % 2] = lax.dot_general(
+            left_ref[left_from + i * TILE : left_from + (i + 1) * TILE, :],
+            right_ref[HEAD : HEAD + n, :],
             (((1,), (1,)), ((), ())),
             preferred_element_type=jnp.float32,
         )
@@ -119,30 +143,27 @@
     def reduce(i):
         ups = [None] * len(groups)
         theirs = [jnp.broadcast_to(right_codes[:, g : g + LANES], (8, LANES)) for g in groups]
-        for j in range(i * TILE, (i + 1) * TILE, 8):
-            mine = spread_ref[j : j + 8, :]
-            best = row_acc[j : j + 8, :] if row_acc is not None else None
+        for j in range(0, TILE, 8):
+            at = start + i * TILE + j
+            mine = spread_ref[at : at + 8, :]
+            best = row_acc[at : at + 8, :]
             for k, g in enumerate(groups):
-                part = scores_ref[i % 2, j - i * TILE : j - i * TILE + 8, g : g + LANES]
+                part = scores_ref[i % 2, j : j + 8, g : g + LANES]
                 lower = theirs[k] > mine
-                if row_acc is not None:
-                    best = jnp.maximum(best, jnp.where(lower, part, -1.0))
+                best = jnp.maximum(best, jnp.where(lower, part, -1.0))
                 if col_acc is not None:
                     up = jnp.where(lower, -1.0, part)
                     ups[k] = up if ups[k] is None else jnp.maximum(ups[k], up)
-            if row_acc is not None:
-                row_acc[j : j + 8, :] = best
+            row_acc[at : at + 8, :] = best
         if col_acc is not None:
             for k, g in enumerate(groups):
-                spot = slice(col_from + g, col_from + g + LANES)
-                col_acc[:, spot] = jnp.maximum(col_acc[:, spot], ups[k])
-
-    last = n // TILE - 1
-    multiply(0)
-    for i in range(1, last + 1):
+                col_acc[:, g : g + LANES] = jnp.maximum(col_acc[:, g : g + LANES], ups[k])
+
+    for i in tiles:
         multiply(i)
-        reduce(i - 1)
-    reduce(last)
+        if i > 0:
+            reduce(i - 1)
+    reduce(tiles[-1])
 
 
 def clear(*refs):
@@ -203,7 +224,7 @@
     own = own.wait()
     row = codes(own, n)
     spread(row, own_codes)
-    pair_job(own, own_codes, own, HEAD, row, own_best, None, scores)
+    pair_job(own, HEAD, own_codes, own, row, own_best, None, scores)
     put_rows(own_out, own_best)
 
 
@@ -219,19 +240,19 @@
 
     @pl.when(has_r1)
     def _():
-        pair_job(own, own_codes, r1, HEAD, codes(r1, n), own_best, r1_best, scores)
+        pair_job(own, HEAD, own_codes, r1, codes(r1, n), own_best, r1_best, scores)
 
     held = odd.wait()
 
     @pl.when(~even)
     def _():
         row = codes(held, n)
-        pair_job(own, own_codes, held, HEAD, row, own_best, None, scores)
+        pair_job(own, HEAD, own_codes, held, row, own_best, None, scores)
         spread(row, y_codes)
 
     @pl.when((~even) & has_r1)
     def _():
-        pair_job(held, y_codes, r1, HEAD, codes(r1, n), y_best, r1_best, scores)
+        pair_job(held, HEAD, y_codes, r1, codes(r1, n), y_best, r1_best, scores)
 
     put_rows(own_out, own_best)
     put_rows(y_out, y_best)
@@ -254,14 +275,14 @@
 
     @pl.when(has_r2)
     def _():
-        pair_job(own, own_codes, r2, HEAD, codes(r2, n), own_best, r2_best, scores)
+        pair_job(own, HEAD, own_codes, r2, codes(r2, n), own_best, r2_best, scores)
 
     held = lower.wait()
     upper.wait()
 
     @pl.when(even)
     def _():
-        pair_job(own, own_codes, held, HEAD, codes(held, n), own_best, None, scores)
+        pair_job(own, HEAD, own_codes, held, codes(held, n), own_best, None, scores)
 
     @pl.when(even | late_y)
     def _():
@@ -269,13 +290,13 @@
 
     @pl.when((even & has_r2 & (y == 0)) | late_y)
     def _():
-        pair_job(held, y_codes, r2, HEAD, codes(r2, n), y_best, r2_best, scores)
+        pair_job(held, HEAD, y_codes, r2, codes(r2, n), y_best, r2_best, scores)
 
     r1 = r1.wait()
 
     @pl.when(has_r1)
     def _():
-        pair_job(held, y_codes, r1, HEAD, codes(r1, n), y_best, r1_best, scores)
+        pair_job(held, HEAD, y_codes, r1, codes(r1, n), y_best, r1_best, scores)
 
     put_rows(own_out, own_best)
     put_rows(y_out, y_best, y_in)
@@ -297,7 +318,7 @@
 
     def meet(left, best):
         spread(codes(left, n), left_codes)
-        pair_job(left, left_codes, kin, HEAD, codes(kin, n), best, kin_best, scores)
+        pair_job(left, HEAD, left_codes, kin, codes(kin, n), best, kin_best, scores)
 
     @pl.when(here)
     def _():
@@ -323,8 +344,8 @@
     put_cols(kin_out, kin_best)
 
 
-def gate_kernel(plan, index_ref, own_hbm, ua_hbm, ub_hbm, top_hbm, side_hbm, even_hbm, odd_hbm, own_out, y_out, top_out, side_out, u_out, own_v, ua_v, ub_v, top_v, side_v, y_v, sems, scores, left_codes, own_best, y_best, top_best, side_best, u_best):
-    n = left_codes.shape[0]
+def gate_kernel(plan, index_ref, own_hbm, ua_hbm, ub_hbm, top_hbm, side_hbm, even_hbm, odd_hbm, own_out, y_out, top_out, side_out, u_out, own_v, ua_v, ub_v, top_v, side_v, y_v, sems, scores, u_codes, u_best, own_best, y_best, top_best, side_best):
+    n = u_codes.shape[0]
     half = n // 2
     r, z, y, even = position(plan, index_ref)
     low = (~even) & (z == plan.Z - 2) & (r < plan.R - 1)
@@ -339,14 +360,14 @@
     clear(own_best, y_best, top_best, side_best, u_best)
     own, ua, ub = own.wait(), ua.wait(), ub.wait()
 
-    def meet(left, best):
-        row = codes(ua, n)
-        spread(codes(left, n), left_codes)
-        pair_job(left, left_codes, ua, HEAD, row[:, :half], best, u_best, scores, 0)
-        pair_job(left, left_codes, ub, 0, row[:, half:], best, u_best, scores, half)
+    def meet(right, best):
+        row = codes(right, n)
+        pair_job(ua, HEAD, u_codes, right, row, u_best, best, scores, (0, half))
+        pair_job(ub, 0, u_codes, right, row, u_best, best, scores, (half, n))
 
     @pl.when(here)
     def _():
+        spread(codes(ua, n), u_codes)
         meet(own, own_best)
 
     top, side = top.wait(), side.wait()
@@ -363,11 +384,11 @@
     def _():
         meet(held, y_best)
 
-    put_rows(own_out, own_best)
-    put_rows(y_out, y_best)
-    put_rows(top_out, top_best)
-    put_rows(side_out, side_best)
-    put_cols(u_out, u_best)
+    put_cols(own_out, own_best)
+    put_cols(y_out, y_best)
+    put_cols(top_out, top_best)
+    put_cols(side_out, side_best)
+    put_rows(u_out, u_best)
 
 
 def finish_kernel(plan, index_ref, count_ref, own_0, own_1, own_2, own_3, own_4, second, first, swap, side, kin, gate, top, side_late, swap_late, out_ref):
@@ -388,7 +409,7 @@
     for ref, mine in returns:
         found = jnp.maximum(found, jnp.where(mine, ref[...], -1.0))
     lane = lax.broadcasted_iota(jnp.int32, found.shape, 1)
-    out_ref[...] = jnp.where(lane < count_ref[0], found, -1.0)
+    out_ref[...] = jnp.where(lane < count_ref[0], found, -1.0).reshape(out_ref.shape)
 
 
 SMEM, VMEM, ANY = (pl.BlockSpec(memory_space=m) for m in (pltpu.SMEM, pltpu.VMEM, pl.ANY))
@@ -400,8 +421,10 @@
     held = blocks if held is None else held
     scratch = [pltpu.VMEM(b.shape, b.dtype) for b in held] + [pltpu.SemaphoreType.DMA((len(blocks),)), pltpu.VMEM((2, TILE, n), jnp.float32)]
     scratch += [pltpu.VMEM((n, LANES), jnp.float32)] * (spreads + rows) + [pltpu.VMEM((8, n), jnp.float32)] * cols
+    used = sum(math.prod(b.shape) * 2 for b in held) + 4 * n * (2 * TILE + LANES * (spreads + rows) + 8 * cols)
     return pl.pallas_call(
         functools.partial(kernel, plan),
+        compiler_params=pltpu.CompilerParams(vmem_limit_bytes=used + SPARE),
         out_shape=[vector] * outs,
         in_specs=[SMEM] + [ANY] * len(blocks) + [VMEM] * len(vectors),
         out_specs=[VMEM] * outs,
@@ -421,11 +444,17 @@
     own = pl.pallas_call(
         functools.partial(pack_kernel, docs),
         out_shape=jax.ShapeDtypeStruct((HEAD + n, width), jnp.bfloat16),
-        in_specs=[SMEM, VMEM, VMEM],
-        out_specs=VMEM,
+        in_specs=[SMEM, ANY, VMEM],
+        out_specs=ANY,
+        scratch_shapes=[
+            pltpu.VMEM((n, width), jnp.bfloat16),
+            pltpu.VMEM((HEAD + n, width), jnp.bfloat16),
+            pltpu.SemaphoreType.DMA((PARTS,)),
+            pltpu.SemaphoreType.DMA((PARTS + 1,)),
+        ],
         cost_estimate=pl.CostEstimate(flops=4 * n * width, bytes_accessed=4 * n * width, transcendentals=n),
         name="pack",
-    )(valid_counts, embeddings, doc_ids.reshape(1, n))
+    )(valid_counts, embeddings, doc_ids)
 
     r1 = permute(own, plan.first)
     odd = permute(own, plan.swap_odd)
@@ -444,7 +473,7 @@
     ub = permute(moved_b, plan.gate_b)
     own_2, y_2, r1_2, r2_2 = stage(second_kernel, plan, at, [own, r2, even, r1, odd], [y_1, r1_1], n, 4, 2, 2, 2, 4, held=[own, r2, even, r1])
     own_3, y_3, r1_3, side_3, kin_3 = stage(kin_kernel, plan, at, [own, kin, r1, side, odd], [y_2, r1_2], n, 5, 1, 4, 1, 4)
-    own_4, y_4, top_4, side_4, u_4 = stage(gate_kernel, plan, at, [own, ua, ub, top, side, even, odd], [], n, 5, 1, 4, 1, 4, held=[own, ua, ub, top, side, even])
+    own_4, y_4, top_4, side_4, u_4 = stage(gate_kernel, plan, at, [own, ua, ub, top, side, even, odd], [], n, 5, 1, 1, 4, 4, held=[own, ua, ub, top, side, even])
 
     returned = [
         permute(r2_2, plan.second_back),
@@ -459,12 +488,13 @@
     ]
     nearest = pl.pallas_call(
         functools.partial(finish_kernel, plan),
-        out_shape=jax.ShapeDtypeStruct((1, n), jnp.float32),
+        out_shape=jax.ShapeDtypeStruct((n,), jnp.float32),
         in_specs=[SMEM, SMEM] + [VMEM] * 14,
         out_specs=VMEM,
+        compiler_params=pltpu.CompilerParams(vmem_limit_bytes=SPARE),
         name="finish",
     )(at, valid_counts, own_0, own_1, own_2, own_3, own_4, *returned)
-    return nearest.reshape(n)
+    return nearest
 
 
 def solution(mesh):

time: 101 us -> 92.5 us (0.916)
  Pallas kernels: 25.9 us -> 17.3 us
  starting transfers between devices: 40.1 us -> 41.4 us
  other arithmetic: 1.28 us -> 0 us
  local copies, waits for them, and re-layouts: 3.13 us -> 4.16 us
    pallas_call x5, Pallas kernels: 21.1 us -> 13.3 us  [stage(): pl.pallas_call(functools.partial(kernel, plan), compiler_params=pltpu.Com...]
    slice x2, local copies, waits for them, and re-layouts: 1.25 us -> 4.15 us  [body(): own_a, moved_b = (own[:half], moved[half:])]
    pallas_call x1 -> x0, other arithmetic: 1.28 us -> none  [body(): pl.pallas_call(functools.partial(finish_kernel, plan), out_shape=jax.Shap...]
    ppermute x19, starting transfers between devices: 40.1 us -> 41.4 us  [permute(): return lax.ppermute(block, AXES, pairs)]
    reshape x1 -> x0, local copies, waits for them, and re-layouts: 1.27 us -> none  [body(): doc_ids.reshape(1, n)]
  transfers between devices with their start and end apart: 19 -> 19, of which waited for: 2 -> 3; matrix products, arithmetic and copies ran while one was open for 1% -> 5% of each run, Pallas kernels for 21% -> 14%
where the time goes in v1:
time: 92.5 us; the launch traced here: 92 us
  starting transfers between devices  41.4 us (45%)
  waiting for transfers between devices  28.2 us (30%)
  Pallas kernels  17.3 us (19%)
  local copies, waits for them, and re-layouts  4.16 us (4%)
    ppermute x19, starting transfers between devices, permute(): return lax.ppermute(block, AXES, pairs)  41.4 us
    ppermute x19, waiting for transfers between devices, permute(): return lax.ppermute(block, AXES, pairs)  28.2 us
    pallas_call x5, Pallas kernels, stage(): pl.pallas_call(functools.partial(kernel, plan), compiler_params=pltpu.Com...  13.3 us
    slice x2, local copies, waits for them, and re-layouts, body(): own_a, moved_b = (own[:half], moved[half:])  4.15 us
    pallas_call x1, Pallas kernels, body(): pl.pallas_call(functools.partial(pack_kernel, docs), out_shape=jax.ShapeD...  3.32 us
  transfers between devices with their start and end apart: 19, of which 3 were waited for; matrix products, arithmetic and copies ran while one was open for 5% of the time, Pallas kernels for 14%

profile of v1, /device:TPU:2, one launch (start us, length us, event | category | flops | bytes accessed | tf_op | source)
XLA Modules:
  0.0 92.0 jit_solution(13523986117783405294)
XLA Ops:
  0.7 3.3 %pack.1.own_hbm = bf16[784,1024]{1,0:T(8,128)(2,1)} custom-call(s32[1]{0:T(128)S(6)} %copy.4.count_ref, bf16[768,1024]{1,0:T(8,128)(2,1)} %emb_hbm.1, s32[768]{0:T(1024)} %ids_ref.1), custom_call_target="tpu_custom_call" | custom-call | flops 3145728 | bytes 3145728 | tf_op jit(solution)/shard_map/pack/pallas_call | solution.py:444
  4.0 0.0 copy-start
  4.0 1.4 %collective-permute-start = (bf16[784,1024]{1,0:T(8,128)(2,1)}, bf16[784,1024]{1,0:T(8,128)(2,1)S(1)}, u32[]{:S(2)}, u32[]{:S(2)}) collective-permute-start(bf16[784,1024]{1,0:T(8,128)(2,1)} %pack.1.own_hbm), channel_id=1, source_target_pairs={{2,0},{3,1},{4,2},{5,3},{6,4},{7,5},{18,16},{19,17},{20,18},{21,19... | collective-permute-start | bytes 4816904 | tf_op jit(solution)/shard_map/ppermute | solution.py:67
  5.4 1.8 %collective-permute-start.1 = (bf16[784,1024]{1,0:T(8,128)(2,1)}, bf16[784,1024]{1,0:T(8,128)(2,1)}, u32[]{:S(2)}, u32[]{:S(2)}) collective-permute-start(bf16[784,1024]{1,0:T(8,128)(2,1)} %pack.1.own_hbm), channel_id=1, source_target_pairs={{8,9},{9,8},{10,11},{11,10},{12,13},{13,12},{14,15},{15,14},{24,25... | collective-permute-start | bytes 4816904 | tf_op jit(solution)/shard_map/ppermute | solution.py:67
  7.3 6.3 %collective-permute-start.6 = (bf16[784,1024]{1,0:T(8,128)(2,1)}, bf16[784,1024]{1,0:T(8,128)(2,1)}, u32[]{:S(2)}, u32[]{:S(2)}) collective-permute-start(bf16[784,1024]{1,0:T(8,128)(2,1)} %pack.1.own_hbm), channel_id=1, source_target_pairs={{14,22},{15,23},{16,8},{17,9}} | collective-permute-start | bytes 4816904 | tf_op jit(solution)/shard_map/ppermute | solution.py:67
  13.6 13.4 %collective-permute-done.r1_hbm = bf16[784,1024]{1,0:T(8,128)(2,1)S(1)} collective-permute-done((bf16[784,1024]{1,0:T(8,128)(2,1)}, bf16[784,1024]{1,0:T(8,128)(2,1)S(1)}, u32[]{:S(2)}, u32[]{:S(2)}) %collective-permute-start) | collective-permute-done | bytes 1605664 | tf_op jit(solution)/shard_map/ppermute | solution.py:67
  27.0 1.3 %collective-permute-start.2 = (bf16[784,1024]{1,0:T(8,128)(2,1)S(1)}, bf16[784,1024]{1,0:T(8,128)(2,1)}, u32[]{:S(2)}, u32[]{:S(2)}) collective-permute-start(bf16[784,1024]{1,0:T(8,128)(2,1)S(1)} %collective-permute-done.r1_hbm), channel_id=1, source_target_pairs={{2,0},{3,1},{4,2},{5,3},{18,16},{19,17},{20,18},{21,19},{10,12},{1... | collective-permute-start | bytes 4816904 | tf_op jit(solution)/shard_map/ppermute | solution.py:67
  28.3 3.4 %collective-permute-start.3 = (bf16[784,1024]{1,0:T(8,128)(2,1)}, bf16[784,1024]{1,0:T(8,128)(2,1)}, u32[]{:S(2)}, u32[]{:S(2)}) collective-permute-start(bf16[784,1024]{1,0:T(8,128)(2,1)} %pack.1.own_hbm), channel_id=1, source_target_pairs={{0,1},{1,0},{2,3},{3,2},{4,5},{5,4},{6,7},{7,6},{16,17},{17,16},{1... | collective-permute-start | bytes 4816904 | tf_op jit(solution)/shard_map/ppermute | solution.py:67
  31.7 0.0 collective-permute-done.1.odd_hbm
  31.7 1.9 %collective-permute-start.5 = (bf16[784,1024]{1,0:T(8,128)(2,1)}, bf16[784,1024]{1,0:T(8,128)(2,1)}, u32[]{:S(2)}, u32[]{:S(2)}) collective-permute-start(bf16[784,1024]{1,0:T(8,128)(2,1)} %collective-permute-done.1.odd_hbm), channel_id=1, source_target_pairs={{8,10},{9,11},{24,26},{25,27},{14,12},{15,13}} | collective-permute-start | bytes 4816904 | tf_op jit(solution)/shard_map/ppermute | solution.py:67
  33.6 0.0 collective-permute-done.6
  33.6 1.9 %collective-permute-start.9 = (bf16[784,1024]{1,0:T(8,128)(2,1)}, bf16[784,1024]{1,0:T(8,128)(2,1)}, u32[]{:S(2)}, u32[]{:S(2)}) collective-permute-start(bf16[784,1024]{1,0:T(8,128)(2,1)} %collective-permute-done.6), channel_id=1, source_target_pairs={{22,12},{23,13}} | collective-permute-start | bytes 4816904 | tf_op jit(solution)/shard_map/ppermute | solution.py:67
  35.5 14.3 %collective-permute-done.2.r2_hbm = bf16[784,1024]{1,0:T(8,128)(2,1)} collective-permute-done((bf16[784,1024]{1,0:T(8,128)(2,1)S(1)}, bf16[784,1024]{1,0:T(8,128)(2,1)}, u32[]{:S(2)}, u32[]{:S(2)}) %collective-permute-start.2) | collective-permute-done | bytes 1605664 | tf_op jit(solution)/shard_map/ppermute | solution.py:67
  49.8 2.5 %collective-permute-start.4 = (bf16[784,1024]{1,0:T(8,128)(2,1)}, bf16[784,1024]{1,0:T(8,128)(2,1)}, u32[]{:S(2)}, u32[]{:S(2)}) collective-permute-start(bf16[784,1024]{1,0:T(8,128)(2,1)} %collective-permute-done.2.r2_hbm), channel_id=1, source_target_pairs={{0,8},{1,9},{16,24},{17,25},{2,10},{3,11},{18,26},{19,27}} | collective-permute-start | bytes 4816904 | tf_op jit(solution)/shard_map/ppermute | solution.py:67
  52.3 2.1 %slice.8 = bf16[400,1024]{1,0:T(8,128)(2,1)} slice(bf16[784,1024]{1,0:T(8,128)(2,1)} %pack.1.own_hbm), slice={[0:400], [0:1024]} | slice | bytes 1638400 | tf_op jit(solution)/shard_map/slice | solution.py:463
  54.4 2.1 %slice.9 = bf16[384,1024]{1,0:T(8,128)(2,1)} slice(bf16[784,1024]{1,0:T(8,128)(2,1)} %collective-permute-done.6), slice={[400:784], [0:1024]} | slice | bytes 1572864 | tf_op jit(solution)/shard_map/slice | solution.py:463
  56.4 2.5 %collective-permute-start.7 = (bf16[400,1024]{1,0:T(8,128)(2,1)}, bf16[400,1024]{1,0:T(8,128)(2,1)}, u32[]{:S(2)}, u32[]{:S(2)}) collective-permute-start(bf16[400,1024]{1,0:T(8,128)(2,1)} %slice.8), channel_id=1, source_target_pairs={{16,12},{17,13},{14,18},{15,19}} | collective-permute-start | bytes 2457608 | tf_op jit(solution)/shard_map/ppermute | solution.py:67
  58.9 0.0 collective-permute-done.3.even_hbm
  58.9 0.7 collective-permute-start.8
  59.6 2.4 %shard_map.38 = (f32[1,768]{1,0:T(1,128)S(1)}, f32[1,768]{1,0:T(1,128)S(1)}, f32[1,768]{1,0:T(1,128)S(1)}) custom-call(s32[1]{0:T(128)} %bitcast.index_ref, bf16[784,1024]{1,0:T(8,128)(2,1)S(1)} %copy-done, bf16[784,1024]{1,0:T(8,128)(2,1)S(1)} %collective-permute-done.r1_hbm, bf16[784,1024]{1,0:T(8,128)(2,1)} %collective-permute-done.1.odd_hbm), custom_call_target="tpu_custom_call" | custom-call | flops 3623878656 | bytes 4718592 | tf_op jit(solution)/shard_map/pallas_call | solution.py:425
  62.0 8.1 %shard_map.39 = (f32[1,768]{1,0:T(1,128)S(1)}, f32[1,768]{1,0:T(1,128)S(1)}, f32[1,768]{1,0:T(1,128)S(1)}, f32[1,768]{1,0:T(1,128)S(1)}) custom-call(s32[1]{0:T(128)} %bitcast.index_ref, bf16[784,1024]{1,0:T(8,128)(2,1)S(1)} %copy-done, bf16[784,1024]{1,0:T(8,128)(2,1)} %collective-permute-done.2.r2_hbm, bf16[784,1024]{1,0:T(8,128)(2,1)} %collective-permute-done.3.even_hbm, ...), custom_call_target="tpu_custom_call" | custom-call | flops 4831838208 | bytes 7864320 | tf_op jit(solution)/shard_map/pallas_call | solution.py:425
  70.1 0.0 collective-permute-done.5.side_hbm
  70.1 1.3 %collective-permute-start.10 = (f32[1,768]{1,0:T(1,128)S(1)}, f32[1,768]{1,0:T(1,128)S(1)}, u32[]{:S(2)}, u32[]{:S(2)}) collective-permute-start(f32[1,768]{1,0:T(1,128)S(1)} %get-tuple-element.36), channel_id=1, source_target_pairs={{0,4},{1,5},{2,6},{3,7},{16,20},{17,21},{18,22},{19,23},{12,8},{13... | collective-permute-start | bytes 9224 | tf_op jit(solution)/shard_map/ppermute | solution.py:67
  71.4 0.0 collective-permute-done.9.top_hbm
  71.4 0.0 collective-permute-done.8.ub_hbm
  71.5 0.0 collective-permute-done.7.ua_hbm
  71.5 0.5 shard_map.41
  72.0 1.3 %collective-permute-start.15 = (f32[1,768]{1,0:T(1,128)S(1)}, f32[1,768]{1,0:T(1,128)S(1)}, u32[]{:S(2)}, u32[]{:S(2)}) collective-permute-start(f32[1,768]{1,0:T(1,128)S(1)} %get-tuple-element.41), channel_id=1, source_target_pairs={{12,16},{13,17},{18,14},{19,15}} | collective-permute-start | bytes 9224 | tf_op jit(solution)/shard_map/ppermute | solution.py:67
  73.3 0.7 collective-permute-start.16
  73.9 0.7 collective-permute-start.17
  74.6 0.0 collective-permute-done.4.kin_hbm
  74.6 0.7 collective-permute-start.18
  75.3 0.7 shard_map.40
  76.0 0.0 collective-permute-done.10.second
  76.0 11.7 %collective-permute-start.11 = (f32[1,768]{1,0:T(1,128)S(1)}, f32[1,768]{1,0:T(1,128)S(1)}, u32[]{:S(2)}, u32[]{:S(2)}) collective-permute-start(f32[1,768]{1,0:T(1,128)S(1)} %get-tuple-element.37), channel_id=1, source_target_pairs={{0,2},{1,3},{2,4},{3,5},{4,6},{5,7},{16,18},{17,19},{18,20},{19,21... | collective-permute-start | bytes 9224 | tf_op jit(solution)/shard_map/ppermute | solution.py:67
  87.7 0.0 collective-permute-done.15.gate
  87.7 0.1 collective-permute-start.12
  87.8 0.0 collective-permute-done.16.top
  87.8 0.7 collective-permute-start.13
  88.4 0.0 collective-permute-done.17.side_late
  88.4 0.7 collective-permute-start.14
  89.1 1.7 %shard_map.37.own_0 = f32[1,768]{1,0:T(1,128)S(1)} custom-call(s32[1]{0:T(128)} %bitcast.index_ref, bf16[784,1024]{1,0:T(8,128)(2,1)S(1)} %copy-done), custom_call_target="tpu_custom_call" | custom-call | flops 1207959552 | bytes 1572864 | tf_op jit(solution)/shard_map/pallas_call | solution.py:425
  90.8 0.0 collective-permute-done.18.swap_late
  90.8 0.0 collective-permute-done.11.first
  90.8 0.5 collective-permute-done.12.swap
  91.3 0.0 collective-permute-done.13.side
  91.3 0.0 collective-permute-done.14.kin
  91.3 0.6 finish.1
  (1 shorter events, 0.0 us)
Async XLA Ops:
  4.0 55.6 %copy-start = (bf16[784,1024]{1,0:T(8,128)(2,1)S(1)}, bf16[784,1024]{1,0:T(8,128)(2,1)}, u32[]{:S(2)}) copy-start(bf16[784,1024]{1,0:T(8,128)(2,1)} %pack.1.own_hbm) | copy-start | bytes 4816900
  4.0 23.0 %collective-permute-start = (bf16[784,1024]{1,0:T(8,128)(2,1)}, bf16[784,1024]{1,0:T(8,128)(2,1)S(1)}, u32[]{:S(2)}, u32[]{:S(2)}) collective-permute-start(bf16[784,1024]{1,0:T(8,128)(2,1)} %pack.1.own_hbm), channel_id=1, source_target_pairs={{2,0},{3,1},{4,2},{5,3},{6,4},{7,5},{18,16},{19,17},{20,18},{21,19... | collective-permute-start | bytes 4816904 | tf_op jit(solution)/shard_map/ppermute | solution.py:67
  5.4 26.3 %collective-permute-start.1 = (bf16[784,1024]{1,0:T(8,128)(2,1)}, bf16[784,1024]{1,0:T(8,128)(2,1)}, u32[]{:S(2)}, u32[]{:S(2)}) collective-permute-start(bf16[784,1024]{1,0:T(8,128)(2,1)} %pack.1.own_hbm), channel_id=1, source_target_pairs={{8,9},{9,8},{10,11},{11,10},{12,13},{13,12},{14,15},{15,14},{24,25... | collective-permute-start | bytes 4816904 | tf_op jit(solution)/shard_map/ppermute | solution.py:67
  7.3 26.3 %collective-permute-start.6 = (bf16[784,1024]{1,0:T(8,128)(2,1)}, bf16[784,1024]{1,0:T(8,128)(2,1)}, u32[]{:S(2)}, u32[]{:S(2)}) collective-permute-start(bf16[784,1024]{1,0:T(8,128)(2,1)} %pack.1.own_hbm), channel_id=1, source_target_pairs={{14,22},{15,23},{16,8},{17,9}} | collective-permute-start | bytes 4816904 | tf_op jit(solution)/shard_map/ppermute | solution.py:67
  27.0 22.8 %collective-permute-start.2 = (bf16[784,1024]{1,0:T(8,128)(2,1)S(1)}, bf16[784,1024]{1,0:T(8,128)(2,1)}, u32[]{:S(2)}, u32[]{:S(2)}) collective-permute-start(bf16[784,1024]{1,0:T(8,128)(2,1)S(1)} %collective-permute-done.r1_hbm), channel_id=1, source_target_pairs={{2,0},{3,1},{4,2},{5,3},{18,16},{19,17},{20,18},{21,19},{10,12},{1... | collective-permute-start | bytes 4816904 | tf_op jit(solution)/shard_map/ppermute | solution.py:67
  28.3 30.6 %collective-permute-start.3 = (bf16[784,1024]{1,0:T(8,128)(2,1)}, bf16[784,1024]{1,0:T(8,128)(2,1)}, u32[]{:S(2)}, u32[]{:S(2)}) collective-permute-start(bf16[784,1024]{1,0:T(8,128)(2,1)} %pack.1.own_hbm), channel_id=1, source_target_pairs={{0,1},{1,0},{2,3},{3,2},{4,5},{5,4},{6,7},{7,6},{16,17},{17,16},{1... | collective-permute-start | bytes 4816904 | tf_op jit(solution)/shard_map/ppermute | solution.py:67
  31.7 38.4 %collective-permute-start.5 = (bf16[784,1024]{1,0:T(8,128)(2,1)}, bf16[784,1024]{1,0:T(8,128)(2,1)}, u32[]{:S(2)}, u32[]{:S(2)}) collective-permute-start(bf16[784,1024]{1,0:T(8,128)(2,1)} %collective-permute-done.1.odd_hbm), channel_id=1, source_target_pairs={{8,10},{9,11},{24,26},{25,27},{14,12},{15,13}} | collective-permute-start | bytes 4816904 | tf_op jit(solution)/shard_map/ppermute | solution.py:67
  33.6 37.8 %collective-permute-start.9 = (bf16[784,1024]{1,0:T(8,128)(2,1)}, bf16[784,1024]{1,0:T(8,128)(2,1)}, u32[]{:S(2)}, u32[]{:S(2)}) collective-permute-start(bf16[784,1024]{1,0:T(8,128)(2,1)} %collective-permute-done.6), channel_id=1, source_target_pairs={{22,12},{23,13}} | collective-permute-start | bytes 4816904 | tf_op jit(solution)/shard_map/ppermute | solution.py:67
  49.8 24.9 %collective-permute-start.4 = (bf16[784,1024]{1,0:T(8,128)(2,1)}, bf16[784,1024]{1,0:T(8,128)(2,1)}, u32[]{:S(2)}, u32[]{:S(2)}) collective-permute-start(bf16[784,1024]{1,0:T(8,128)(2,1)} %collective-permute-done.2.r2_hbm), channel_id=1, source_target_pairs={{0,8},{1,9},{16,24},{17,25},{2,10},{3,11},{18,26},{19,27}} | collective-permute-start | bytes 4816904 | tf_op jit(solution)/shard_map/ppermute | solution.py:67
  56.4 15.0 %collective-permute-start.7 = (bf16[400,1024]{1,0:T(8,128)(2,1)}, bf16[400,1024]{1,0:T(8,128)(2,1)}, u32[]{:S(2)}, u32[]{:S(2)}) collective-permute-start(bf16[400,1024]{1,0:T(8,128)(2,1)} %slice.8), channel_id=1, source_target_pairs={{16,12},{17,13},{14,18},{15,19}} | collective-permute-start | bytes 2457608 | tf_op jit(solution)/shard_map/ppermute | solution.py:67
  58.9 12.5 %collective-permute-start.8 = (bf16[384,1024]{1,0:T(8,128)(2,1)}, bf16[384,1024]{1,0:T(8,128)(2,1)S(1)}, u32[]{:S(2)}, u32[]{:S(2)}) collective-permute-start(bf16[384,1024]{1,0:T(8,128)(2,1)} %slice.9), channel_id=1, source_target_pairs={{8,12},{9,13},{22,18},{23,19}} | collective-permute-start | bytes 2359304 | tf_op jit(solution)/shard_map/ppermute | solution.py:67
  70.1 5.8 %collective-permute-start.10 = (f32[1,768]{1,0:T(1,128)S(1)}, f32[1,768]{1,0:T(1,128)S(1)}, u32[]{:S(2)}, u32[]{:S(2)}) collective-permute-start(f32[1,768]{1,0:T(1,128)S(1)} %get-tuple-element.36), channel_id=1, source_target_pairs={{0,4},{1,5},{2,6},{3,7},{16,20},{17,21},{18,22},{19,23},{12,8},{13... | collective-permute-start | bytes 9224 | tf_op jit(solution)/shard_map/ppermute | solution.py:67
  72.0 15.7 %collective-permute-start.15 = (f32[1,768]{1,0:T(1,128)S(1)}, f32[1,768]{1,0:T(1,128)S(1)}, u32[]{:S(2)}, u32[]{:S(2)}) collective-permute-start(f32[1,768]{1,0:T(1,128)S(1)} %get-tuple-element.41), channel_id=1, source_target_pairs={{12,16},{13,17},{18,14},{19,15}} | collective-permute-start | bytes 9224 | tf_op jit(solution)/shard_map/ppermute | solution.py:67
  73.3 14.5 %collective-permute-start.16 = (f32[1,768]{1,0:T(1,128)S(1)}, f32[1,768]{1,0:T(1,128)S(1)}, u32[]{:S(2)}, u32[]{:S(2)}) collective-permute-start(f32[1,768]{1,0:T(1,128)S(1)} %get-tuple-element.42), channel_id=1, source_target_pairs={{12,14},{13,15}} | collective-permute-start | bytes 9224 | tf_op jit(solution)/shard_map/ppermute | solution.py:67
  73.9 14.5 %collective-permute-start.17 = (f32[1,768]{1,0:T(1,128)S(1)}, f32[1,768]{1,0:T(1,128)S(1)}, u32[]{:S(2)}, u32[]{:S(2)}) collective-permute-start(f32[1,768]{1,0:T(1,128)S(1)} %get-tuple-element.43), channel_id=1, source_target_pairs={{12,15},{13,14}} | collective-permute-start | bytes 9224 | tf_op jit(solution)/shard_map/ppermute | solution.py:67
  74.6 16.2 %collective-permute-start.18 = (f32[1,768]{1,0:T(1,128)S(1)}, f32[1,768]{1,0:T(1,128)S(1)}, u32[]{:S(2)}, u32[]{:S(2)}) collective-permute-start(f32[1,768]{1,0:T(1,128)S(1)} %get-tuple-element.44), channel_id=1, source_target_pairs={{12,13},{13,12},{18,19},{19,18}} | collective-permute-start | bytes 9224 | tf_op jit(solution)/shard_map/ppermute | solution.py:67
  76.0 14.8 %collective-permute-start.11 = (f32[1,768]{1,0:T(1,128)S(1)}, f32[1,768]{1,0:T(1,128)S(1)}, u32[]{:S(2)}, u32[]{:S(2)}) collective-permute-start(f32[1,768]{1,0:T(1,128)S(1)} %get-tuple-element.37), channel_id=1, source_target_pairs={{0,2},{1,3},{2,4},{3,5},{4,6},{5,7},{16,18},{17,19},{18,20},{19,21... | collective-permute-start | bytes 9224 | tf_op jit(solution)/shard_map/ppermute | solution.py:67
  87.7 3.7 %collective-permute-start.12 = (f32[1,768]{1,0:T(1,128)S(1)}, f32[1,768]{1,0:T(1,128)S(1)}, u32[]{:S(2)}, u32[]{:S(2)}) collective-permute-start(f32[1,768]{1,0:T(1,128)S(1)} %get-tuple-element.38), channel_id=1, source_target_pairs={{0,1},{1,0},{2,3},{3,2},{4,5},{5,4},{6,7},{7,6},{16,17},{17,16},{1... | collective-permute-start | bytes 9224 | tf_op jit(solution)/shard_map/ppermute | solution.py:67
  87.8 3.6 %collective-permute-start.13 = (f32[1,768]{1,0:T(1,128)S(1)}, f32[1,768]{1,0:T(1,128)S(1)}, u32[]{:S(2)}, u32[]{:S(2)}) collective-permute-start(f32[1,768]{1,0:T(1,128)S(1)} %get-tuple-element.39), channel_id=1, source_target_pairs={{10,9},{11,8},{26,25},{27,24}} | collective-permute-start | bytes 9224 | tf_op jit(solution)/shard_map/ppermute | solution.py:67
  88.4 2.9 %collective-permute-start.14 = (f32[1,768]{1,0:T(1,128)S(1)}, f32[1,768]{1,0:T(1,128)S(1)}, u32[]{:S(2)}, u32[]{:S(2)}) collective-permute-start(f32[1,768]{1,0:T(1,128)S(1)} %get-tuple-element.40), channel_id=1, source_target_pairs={{8,4},{9,5},{24,20},{25,21},{10,6},{11,7},{26,22},{27,23}} | collective-permute-start | bytes 9224 | tf_op jit(solution)/shard_map/ppermute | solution.py:67

commit v2 on v1

--- a/solution.py
+++ b/solution.py
@@ -45,15 +45,14 @@
         self.first_back = [(b, a) for a, b in self.first]
         self.second_back = [(at(r, z, y), at(r, z + 2, y)) for r in even for z in range(Z - 2) for y in ys]
         self.second_back += [(at(r, z, y), at(r, z - 2, y)) for r in odd for z in range(2, Z) for y in ys]
-        self.kin_back = [(at(r + 1, 0, y), at(r, Z - 2, y)) for r in even for y in ys]
-        self.kin_back += [(at(r + 1, 1, y), at(r, Z - 1, y)) for r in even for y in ys]
         self.side_back = [(at(r, 1, y), at(r, 0, 1 - y)) for r in odd for y in ys]
-        self.side_back_late = [(at(r, Z - 2, y), at(r, Z - 1, 1 - y)) for r in gate for y in ys]
-        self.top_back = [(at(r, Z - 2, y), at(r, Z - 1, y)) for r in gate for y in ys]
-        self.gate_back = [(b, a) for a, b in self.gate_a]
+        self.side_back += [(at(r, Z - 2, y), at(r, Z - 1, 1 - y)) for r in gate for y in ys]
+        self.top_back = [(at(r, 1, y), at(r, 0, y)) for r in odd for y in ys]
+        self.top_back += [(at(r, Z - 2, y), at(r, Z - 1, y)) for r in gate for y in ys]
+        self.row_back = [(at(r + 1, 0, y), at(r, Z - 2, y)) for r in even for y in ys]
+        self.row_back += [(at(r + 1, 1, y), at(r, Z - 1, y)) for r in even for y in ys]
+        self.row_back += [(b, a) for a, b in self.gate_a]
         self.swap = self.swap_even + self.swap_odd
-        self.swap_late = [(at(r, Z - 2, y), at(r, Z - 2, 1 - y)) for r in gate for y in ys]
-        self.swap_late += [(at(r + 1, 1, y), at(r + 1, 1, 1 - y)) for r in gate for y in ys]
 
     def at(self, r, z, y):
         return r * self.C + z * Y + y
@@ -228,35 +227,46 @@
     put_rows(own_out, own_best)
 
 
-def first_kernel(plan, index_ref, own_hbm, r1_hbm, odd_hbm, own_out, y_out, r1_out, own_v, r1_v, odd_v, sems, scores, own_codes, y_codes, own_best, y_best, r1_best):
+def first_kernel(plan, index_ref, own_hbm, r1_hbm, own_out, r1_out, own_v, r1_v, sems, scores, own_codes, own_best, r1_best):
     n = own_codes.shape[0]
     _, z, _, even = position(plan, index_ref)
     has_r1 = jnp.where(even, z <= plan.Z - 2, z >= 1)
-    own, r1, odd = fetches([own_hbm, r1_hbm, odd_hbm], [own_v, r1_v, odd_v], sems, [True, has_r1, ~even])
-    clear(own_best, y_best, r1_best)
-    own = own.wait()
-    spread(codes(own, n), own_codes)
+    own, r1 = fetches([own_hbm, r1_hbm], [own_v, r1_v], sems, [has_r1, has_r1])
+    clear(own_best, r1_best)
+    own, r1 = own.wait(), r1.wait()
+
+    @pl.when(has_r1)
+    def _():
+        spread(codes(own, n), own_codes)
+        pair_job(own, HEAD, own_codes, r1, codes(r1, n), own_best, r1_best, scores)
+
+    put_rows(own_out, own_best)
+    put_cols(r1_out, r1_best)
+
+
+def cross_kernel(plan, index_ref, own_hbm, odd_hbm, r1_hbm, r1_in, own_out, y_out, r1_out, own_v, odd_v, r1_v, sems, scores, y_codes, y_best, own_best, r1_best):
+    n = y_codes.shape[0]
+    _, z, _, even = position(plan, index_ref)
+    odd = ~even
+    has_r1 = odd & (z >= 1)
+    own, other, r1 = fetches([own_hbm, odd_hbm, r1_hbm], [own_v, odd_v, r1_v], sems, [odd, odd, has_r1])
+    clear(y_best, own_best, r1_best)
+    own, other = own.wait(), other.wait()
+
+    @pl.when(odd)
+    def _():
+        spread(codes(other, n), y_codes)
+        pair_job(other, HEAD, y_codes, own, codes(own, n), y_best, own_best, scores)
+
     r1 = r1.wait()
 
     @pl.when(has_r1)
     def _():
-        pair_job(own, HEAD, own_codes, r1, codes(r1, n), own_best, r1_best, scores)
-
-    held = odd.wait()
-
-    @pl.when(~even)
-    def _():
-        row = codes(held, n)
-        pair_job(own, HEAD, own_codes, held, row, own_best, None, scores)
-        spread(row, y_codes)
-
-    @pl.when((~even) & has_r1)
-    def _():
-        pair_job(held, HEAD, y_codes, r1, codes(r1, n), y_best, r1_best, scores)
-
-    put_rows(own_out, own_best)
+        pair_job(other, HEAD, y_codes, r1, codes(r1, n), y_best, r1_best, scores)
+
+    put_cols(own_out, own_best)
     put_rows(y_out, y_best)
-    put_cols(r1_out, r1_best)
+    put_cols(r1_out, r1_best, r1_in)
 
 
 def second_kernel(plan, index_ref, own_hbm, r2_hbm, even_hbm, r1_hbm, odd_hbm, y_in, r1_in, own_out, y_out, r1_out, r2_out, own_v, r2_v, y_v, r1_v, sems, scores, own_codes, y_codes, own_best, y_best, r1_best, r2_best):
@@ -304,7 +314,7 @@
     put_cols(r2_out, r2_best)
 
 
-def kin_kernel(plan, index_ref, own_hbm, kin_hbm, r1_hbm, side_hbm, odd_hbm, y_in, r1_in, own_out, y_out, r1_out, side_out, kin_out, own_v, kin_v, r1_v, side_v, odd_v, sems, scores, left_codes, own_best, y_best, r1_best, side_best, kin_best):
+def kin_kernel(plan, index_ref, own_hbm, kin_hbm, r1_hbm, side_hbm, odd_hbm, y_in, own_out, y_out, r1_out, side_out, kin_out, own_v, kin_v, r1_v, side_v, odd_v, sems, scores, left_codes, own_best, y_best, r1_best, side_best, kin_best):
     n = left_codes.shape[0]
     _, z, y, even = position(plan, index_ref)
     here = (~even) & (z <= 1)
@@ -339,12 +349,12 @@
 
     put_rows(own_out, own_best)
     put_rows(y_out, y_best, y_in)
-    put_rows(r1_out, r1_best, r1_in)
+    put_rows(r1_out, r1_best)
     put_rows(side_out, side_best)
     put_cols(kin_out, kin_best)
 
 
-def gate_kernel(plan, index_ref, own_hbm, ua_hbm, ub_hbm, top_hbm, side_hbm, even_hbm, odd_hbm, own_out, y_out, top_out, side_out, u_out, own_v, ua_v, ub_v, top_v, side_v, y_v, sems, scores, u_codes, u_best, own_best, y_best, top_best, side_best):
+def gate_kernel(plan, index_ref, own_hbm, ua_hbm, ub_hbm, top_hbm, side_hbm, even_hbm, odd_hbm, y_in, top_in, side_in, u_in, own_out, y_out, top_out, side_out, u_out, own_v, ua_v, ub_v, top_v, side_v, y_v, sems, scores, u_codes, u_best, own_best, y_best, top_best, side_best):
     n = u_codes.shape[0]
     half = n // 2
     r, z, y, even = position(plan, index_ref)
@@ -385,26 +395,23 @@
         meet(held, y_best)
 
     put_cols(own_out, own_best)
-    put_cols(y_out, y_best)
-    put_cols(top_out, top_best)
-    put_cols(side_out, side_best)
-    put_rows(u_out, u_best)
-
-
-def finish_kernel(plan, index_ref, count_ref, own_0, own_1, own_2, own_3, own_4, second, first, swap, side, kin, gate, top, side_late, swap_late, out_ref):
+    put_cols(y_out, y_best, y_in)
+    put_cols(top_out, top_best, top_in)
+    put_cols(side_out, side_best, side_in)
+    put_rows(u_out, u_best, u_in)
+
+
+def finish_kernel(plan, index_ref, count_ref, own_0, own_1, own_2, own_3, own_4, own_5, second, first, row, top, side, swap, out_ref):
     r, z, _, even = position(plan, index_ref)
     Z, R = plan.Z, plan.R
-    found = functools.reduce(jnp.maximum, [ref[...] for ref in (own_0, own_1, own_2, own_3, own_4, swap)])
+    found = functools.reduce(jnp.maximum, [ref[...] for ref in (own_0, own_1, own_2, own_3, own_4, own_5, swap)])
     inner = (~even) & (r < R - 1)
     returns = (
         (second, jnp.where(even, z >= 2, z <= Z - 3)),
         (first, jnp.where(even, z >= 1, z <= Z - 2)),
-        (side, (~even) & (z == 0)),
-        (kin, even & (z >= Z - 2)),
-        (gate, (even & (r >= 2) & (z == 0)) | (inner & (z == Z - 1))),
-        (top, inner & (z == Z - 1)),
-        (side_late, inner & (z == Z - 1)),
-        (swap_late, (inner & (z == Z - 2)) | (even & (r >= 2) & (z == 1))),
+        (row, jnp.where(even, (z >= Z - 2) | ((r >= 2) & (z == 0)), inner & (z == Z - 1))),
+        (top, (~even) & ((z == 0) | (inner & (z == Z - 1)))),
+        (side, (~even) & ((z == 0) | (inner & (z == Z - 1)))),
     )
     for ref, mine in returns:
         found = jnp.maximum(found, jnp.where(mine, ref[...], -1.0))
@@ -460,40 +467,39 @@
     odd = permute(own, plan.swap_odd)
     moved = permute(own, plan.across)
     (own_0,) = stage(self_kernel, plan, at, [own], [], n, 1, 1, 1, 0, 1)
-    own_a, moved_b = own[:half], moved[half:]
+    own_a = own[:half]
+    moved_b = moved[half:]
     r2 = permute(r1, plan.second)
     side = permute(odd, plan.side)
     top = permute(moved, plan.top)
     own_late, _ = lax.optimization_barrier((own, r1))
     even = permute(own_late, plan.swap_even)
-    own_1, y_1, r1_1 = stage(first_kernel, plan, at, [own, r1, odd], [], n, 3, 2, 2, 1, 3)
+    own_1, r1_0 = stage(first_kernel, plan, at, [own, r1], [], n, 2, 1, 1, 1, 1)
+    own_5, y_1, r1_1 = stage(cross_kernel, plan, at, [own, odd, r1], [r1_0], n, 3, 1, 1, 2, 2)
     kin = permute(r2, plan.kin)
     own_a, moved_b, _ = lax.optimization_barrier((own_a, moved_b, r2))
     ua = permute(own_a, plan.gate_a)
     ub = permute(moved_b, plan.gate_b)
     own_2, y_2, r1_2, r2_2 = stage(second_kernel, plan, at, [own, r2, even, r1, odd], [y_1, r1_1], n, 4, 2, 2, 2, 4, held=[own, r2, even, r1])
-    own_3, y_3, r1_3, side_3, kin_3 = stage(kin_kernel, plan, at, [own, kin, r1, side, odd], [y_2, r1_2], n, 5, 1, 4, 1, 4)
-    own_4, y_4, top_4, side_4, u_4 = stage(gate_kernel, plan, at, [own, ua, ub, top, side, even, odd], [], n, 5, 1, 1, 4, 4, held=[own, ua, ub, top, side, even])
+    own_3, y_3, r1_3, side_3, kin_3 = stage(kin_kernel, plan, at, [own, kin, r1, side, odd], [y_2], n, 5, 1, 4, 1, 4)
+    own_4, y_4, top_4, side_4, u_4 = stage(gate_kernel, plan, at, [own, ua, ub, top, side, even, odd], [y_3, r1_3, side_3, kin_3], n, 5, 1, 1, 4, 4, held=[own, ua, ub, top, side, even])
 
     returned = [
         permute(r2_2, plan.second_back),
-        permute(r1_3, plan.first_back),
-        permute(y_3, plan.swap),
-        permute(side_3, plan.side_back),
-        permute(kin_3, plan.kin_back),
-        permute(u_4, plan.gate_back),
+        permute(r1_2, plan.first_back),
+        permute(u_4, plan.row_back),
         permute(top_4, plan.top_back),
-        permute(side_4, plan.side_back_late),
-        permute(y_4, plan.swap_late),
+        permute(side_4, plan.side_back),
+        permute(y_4, plan.swap),
     ]
     nearest = pl.pallas_call(
         functools.partial(finish_kernel, plan),
         out_shape=jax.ShapeDtypeStruct((n,), jnp.float32),
-        in_specs=[SMEM, SMEM] + [VMEM] * 14,
+        in_specs=[SMEM, SMEM] + [VMEM] * 12,
         out_specs=VMEM,
         compiler_params=pltpu.CompilerParams(vmem_limit_bytes=SPARE),
         name="finish",
-    )(at, valid_counts, own_0, own_1, own_2, own_3, own_4, *returned)
+    )(at, valid_counts, own_0, own_1, own_2, own_3, own_4, own_5, *returned)
     return nearest
 
 

time: 92.5 us -> 97.1 us (1.050)
  the two profiles are of different devices: /device:TPU:2 before, /device:TPU:14 now
where the time goes in v2:
time: 97.1 us; the launch traced here: 96.5 us
  waiting for transfers between devices  44 us (45%)
  starting transfers between devices  25.6 us (26%)
  Pallas kernels  19.2 us (20%)
  local copies, waits for them, and re-layouts  6.84 us (7%)
    ppermute x16, waiting for transfers between devices, permute(): return lax.ppermute(block, AXES, pairs)  44 us
    ppermute x16, starting transfers between devices, permute(): return lax.ppermute(block, AXES, pairs)  25.6 us
    pallas_call x6, Pallas kernels, stage(): pl.pallas_call(functools.partial(kernel, plan), compiler_params=pltpu.Com...  15.3 us
    unnamed x10, local copies, waits for them, and re-layouts  3.42 us
    pallas_call x1, Pallas kernels, body(): pl.pallas_call(functools.partial(pack_kernel, docs), out_shape=jax.ShapeD...  3.31 us
    slice x1, local copies, waits for them, and re-layouts, body(): own_a = own[:half]  2.23 us
  transfers between devices with their start and end apart: 16, of which 4 were waited for; matrix products, arithmetic and copies ran while one was open for 4% of the time, Pallas kernels for 16%

profile of v2, /device:TPU:14, one launch (start us, length us, event | category | flops | bytes accessed | tf_op | source)
XLA Modules:
  0.0 96.5 jit_solution(7847603121568301705)
XLA Ops:
  0.7 3.3 %pack.1.own_hbm = bf16[784,1024]{1,0:T(8,128)(2,1)} custom-call(s32[1]{0:T(128)S(6)} %copy.4.count_ref, bf16[768,1024]{1,0:T(8,128)(2,1)} %emb_hbm.1, s32[768]{0:T(1024)} %ids_ref.1), custom_call_target="tpu_custom_call" | custom-call | flops 3145728 | bytes 3145728 | tf_op jit(solution)/shard_map/pack/pallas_call | solution.py:451
  4.0 2.4 %collective-permute-start = (bf16[784,1024]{1,0:T(8,128)(2,1)}, bf16[784,1024]{1,0:T(8,128)(2,1)S(1)}, u32[]{:S(2)}, u32[]{:S(2)}) collective-permute-start(bf16[784,1024]{1,0:T(8,128)(2,1)} %pack.1.own_hbm), channel_id=1, source_target_pairs={{2,0},{3,1},{4,2},{5,3},{6,4},{7,5},{18,16},{19,17},{20,18},{21,19... | collective-permute-start | bytes 4816904 | tf_op jit(solution)/shard_map/ppermute | solution.py:66
  6.3 0.8 collective-permute-start.3
  7.1 19.7 %collective-permute-done.r1_hbm = bf16[784,1024]{1,0:T(8,128)(2,1)S(1)} collective-permute-done((bf16[784,1024]{1,0:T(8,128)(2,1)}, bf16[784,1024]{1,0:T(8,128)(2,1)S(1)}, u32[]{:S(2)}, u32[]{:S(2)}) %collective-permute-start) | collective-permute-done | bytes 1605664 | tf_op jit(solution)/shard_map/ppermute | solution.py:66
  26.8 2.3 %collective-permute-start.1 = (bf16[784,1024]{1,0:T(8,128)(2,1)S(1)}, bf16[784,1024]{1,0:T(8,128)(2,1)}, u32[]{:S(2)}, u32[]{:S(2)}) collective-permute-start(bf16[784,1024]{1,0:T(8,128)(2,1)S(1)} %collective-permute-done.r1_hbm), channel_id=1, source_target_pairs={{2,0},{3,1},{4,2},{5,3},{18,16},{19,17},{20,18},{21,19},{10,12},{1... | collective-permute-start | bytes 4816904 | tf_op jit(solution)/shard_map/ppermute | solution.py:66
  29.2 0.0 copy-start.1
  29.2 1.1 %copy-done.1 = bf16[784,1024]{1,0:T(8,128)(2,1)} copy-done((bf16[784,1024]{1,0:T(8,128)(2,1)}, bf16[784,1024]{1,0:T(8,128)(2,1)S(1)}, u32[]{:S(2)}) %copy-start.1) | copy-done | bytes 1605656
  30.4 1.8 %collective-permute-start.6 = (bf16[784,1024]{1,0:T(8,128)(2,1)}, bf16[784,1024]{1,0:T(8,128)(2,1)}, u32[]{:S(2)}, u32[]{:S(2)}) collective-permute-start(bf16[784,1024]{1,0:T(8,128)(2,1)} %pack.1.own_hbm), channel_id=1, source_target_pairs={{14,22},{15,23},{16,8},{17,9}} | collective-permute-start | bytes 4816904 | tf_op jit(solution)/shard_map/ppermute | solution.py:66
  32.2 2.4 %collective-permute-start.2 = (bf16[784,1024]{1,0:T(8,128)(2,1)}, bf16[784,1024]{1,0:T(8,128)(2,1)}, u32[]{:S(2)}, u32[]{:S(2)}) collective-permute-start(bf16[784,1024]{1,0:T(8,128)(2,1)} %pack.1.own_hbm), channel_id=1, source_target_pairs={{0,1},{1,0},{2,3},{3,2},{4,5},{5,4},{6,7},{7,6},{16,17},{17,16},{1... | collective-permute-start | bytes 4816904 | tf_op jit(solution)/shard_map/ppermute | solution.py:66
  34.6 0.0 collective-permute-done.3.odd_hbm
  34.6 1.9 %collective-permute-start.5 = (bf16[784,1024]{1,0:T(8,128)(2,1)S(1)}, bf16[784,1024]{1,0:T(8,128)(2,1)}, u32[]{:S(2)}, u32[]{:S(2)}) collective-permute-start(bf16[784,1024]{1,0:T(8,128)(2,1)S(1)} %collective-permute-done.3.odd_hbm), channel_id=1, source_target_pairs={{8,10},{9,11},{24,26},{25,27},{14,12},{15,13}} | collective-permute-start | bytes 4816904 | tf_op jit(solution)/shard_map/ppermute | solution.py:66
  36.5 13.1 %collective-permute-done.1.r2_hbm = bf16[784,1024]{1,0:T(8,128)(2,1)} collective-permute-done((bf16[784,1024]{1,0:T(8,128)(2,1)S(1)}, bf16[784,1024]{1,0:T(8,128)(2,1)}, u32[]{:S(2)}, u32[]{:S(2)}) %collective-permute-start.1) | collective-permute-done | bytes 1605664 | tf_op jit(solution)/shard_map/ppermute | solution.py:66
  49.6 2.5 %collective-permute-start.4 = (bf16[784,1024]{1,0:T(8,128)(2,1)}, bf16[784,1024]{1,0:T(8,128)(2,1)}, u32[]{:S(2)}, u32[]{:S(2)}) collective-permute-start(bf16[784,1024]{1,0:T(8,128)(2,1)} %collective-permute-done.1.r2_hbm), channel_id=1, source_target_pairs={{0,8},{1,9},{16,24},{17,25},{2,10},{3,11},{18,26},{19,27}} | collective-permute-start | bytes 4816904 | tf_op jit(solution)/shard_map/ppermute | solution.py:66
  52.1 0.0 collective-permute-done.6
  52.1 1.9 %collective-permute-start.9 = (bf16[784,1024]{1,0:T(8,128)(2,1)}, bf16[784,1024]{1,0:T(8,128)(2,1)}, u32[]{:S(2)}, u32[]{:S(2)}) collective-permute-start(bf16[784,1024]{1,0:T(8,128)(2,1)} %collective-permute-done.6), channel_id=1, source_target_pairs={{22,12},{23,13}} | collective-permute-start | bytes 4816904 | tf_op jit(solution)/shard_map/ppermute | solution.py:66
  54.0 2.2 %slice.8 = bf16[400,1024]{1,0:T(8,128)(2,1)} slice(bf16[784,1024]{1,0:T(8,128)(2,1)} %pack.1.own_hbm), slice={[0:400], [0:1024]} | slice | bytes 1638400 | tf_op jit(solution)/shard_map/slice | solution.py:470
  56.2 1.2 %slice.9 = bf16[384,1024]{1,0:T(8,128)(2,1)S(1)} slice(bf16[784,1024]{1,0:T(8,128)(2,1)} %collective-permute-done.6), slice={[400:784], [0:1024]} | slice | bytes 1572864 | tf_op jit(solution)/shard_map/slice | solution.py:471
  57.4 0.0 copy-done
  57.4 0.0 copy-start.2
  57.4 1.4 %copy-done.2 = bf16[784,1024]{1,0:T(8,128)(2,1)S(1)} copy-done((bf16[784,1024]{1,0:T(8,128)(2,1)S(1)}, bf16[784,1024]{1,0:T(8,128)(2,1)}, u32[]{:S(2)}) %copy-start.2) | copy-done | bytes 1605656
  58.8 2.0 %shard_map.38 = (f32[1,768]{1,0:T(1,128)S(1)}, f32[1,768]{1,0:T(1,128)S(1)}) custom-call(s32[1]{0:T(128)} %bitcast.index_ref, bf16[784,1024]{1,0:T(8,128)(2,1)S(1)} %copy-done, bf16[784,1024]{1,0:T(8,128)(2,1)S(1)} %copy-done.2), custom_call_target="tpu_custom_call" | custom-call | flops 1207959552 | bytes 3145728 | tf_op jit(solution)/shard_map/pallas_call | solution.py:432
  60.9 0.3 shard_map.39
  61.2 0.9 copy-done.4
  62.0 1.3 %collective-permute-start.7 = (bf16[400,1024]{1,0:T(8,128)(2,1)S(1)}, bf16[400,1024]{1,0:T(8,128)(2,1)S(1)}, u32[]{:S(2)}, u32[]{:S(2)}) collective-permute-start(bf16[400,1024]{1,0:T(8,128)(2,1)S(1)} %copy-done.4), channel_id=1, source_target_pairs={{16,12},{17,13},{14,18},{15,19}} | collective-permute-start | bytes 2457608 | tf_op jit(solution)/shard_map/ppermute | solution.py:66
  63.3 0.0 collective-permute-done.2.even_hbm
  63.3 1.3 %collective-permute-start.8 = (bf16[384,1024]{1,0:T(8,128)(2,1)S(1)}, bf16[384,1024]{1,0:T(8,128)(2,1)S(1)}, u32[]{:S(2)}, u32[]{:S(2)}) collective-permute-start(bf16[384,1024]{1,0:T(8,128)(2,1)S(1)} %slice.9), channel_id=1, source_target_pairs={{8,12},{9,13},{22,18},{23,19}} | collective-permute-start | bytes 2359304 | tf_op jit(solution)/shard_map/ppermute | solution.py:66
  64.6 6.7 %shard_map.40 = (f32[1,768]{1,0:T(1,128)S(1)}, f32[1,768]{1,0:T(1,128)S(1)}, f32[1,768]{1,0:T(1,128)S(1)}, f32[1,768]{1,0:T(1,128)S(1)}) custom-call(s32[1]{0:T(128)} %bitcast.index_ref, bf16[784,1024]{1,0:T(8,128)(2,1)S(1)} %copy-done, bf16[784,1024]{1,0:T(8,128)(2,1)} %collective-permute-done.1.r2_hbm, bf16[784,1024]{1,0:T(8,128)(2,1)} %collective-permute-done.2.even_hbm, ...), custom_call_target="tpu_custom_call" | custom-call | flops 4831838208 | bytes 7864320 | tf_op jit(solution)/shard_map/pallas_call | solution.py:432
  71.4 0.0 collective-permute-done.5.side_hbm
  71.4 2.5 %collective-permute-start.10 = (f32[1,768]{1,0:T(1,128)S(1)}, f32[1,768]{1,0:T(1,128)S(1)}, u32[]{:S(2)}, u32[]{:S(2)}) collective-permute-start(f32[1,768]{1,0:T(1,128)S(1)} %get-tuple-element.43), channel_id=1, source_target_pairs={{0,4},{1,5},{2,6},{3,7},{16,20},{17,21},{18,22},{19,23},{12,8},{13... | collective-permute-start | bytes 9224 | tf_op jit(solution)/shard_map/ppermute | solution.py:66
  73.9 0.0 collective-permute-done.4.kin_hbm
  73.9 1.9 %collective-permute-start.11 = (f32[1,768]{1,0:T(1,128)S(1)}, f32[1,768]{1,0:T(1,128)S(1)}, u32[]{:S(2)}, u32[]{:S(2)}) collective-permute-start(f32[1,768]{1,0:T(1,128)S(1)} %get-tuple-element.44), channel_id=1, source_target_pairs={{0,2},{1,3},{2,4},{3,5},{4,6},{5,7},{16,18},{17,19},{18,20},{19,21... | collective-permute-start | bytes 9224 | tf_op jit(solution)/shard_map/ppermute | solution.py:66
  75.8 0.7 shard_map.41
  76.5 0.0 collective-permute-done.9.top_hbm
  76.5 9.2 %collective-permute-done.8.ub_hbm = bf16[384,1024]{1,0:T(8,128)(2,1)S(1)} collective-permute-done((bf16[384,1024]{1,0:T(8,128)(2,1)S(1)}, bf16[384,1024]{1,0:T(8,128)(2,1)S(1)}, u32[]{:S(2)}, u32[]{:S(2)}) %collective-permute-start.8) | collective-permute-done | bytes 786464 | tf_op jit(solution)/shard_map/ppermute | solution.py:66
  85.7 0.0 collective-permute-done.7.ua_hbm
  85.7 3.9 %shard_map.42 = (f32[1,768]{1,0:T(1,128)S(1)}, f32[1,768]{1,0:T(1,128)S(1)}, f32[1,768]{1,0:T(1,128)S(1)}, f32[1,768]{1,0:T(1,128)S(1)}, f32[1,768]{1,0:T(1,128)S(1)}) custom-call(s32[1]{0:T(128)} %bitcast.index_ref, bf16[784,1024]{1,0:T(8,128)(2,1)S(1)} %copy-done, bf16[400,1024]{1,0:T(8,128)(2,1)S(1)} %collective-permute-done.7.ua_hbm, ...), custom_call_target="tpu_custom_call" | custom-call | flops 4831838208 | bytes 11010048 | tf_op jit(solution)/shard_map/pallas_call | solution.py:432
  89.6 1.3 %collective-permute-start.12 = (f32[1,768]{1,0:T(1,128)S(1)}, f32[1,768]{1,0:T(1,128)S(1)}, u32[]{:S(2)}, u32[]{:S(2)}) collective-permute-start(f32[1,768]{1,0:T(1,128)S(1)} %get-tuple-element.45), channel_id=1, source_target_pairs={{8,4},{9,5},{24,20},{25,21},{10,6},{11,7},{26,22},{27,23},{12,16},... | collective-permute-start | bytes 9224 | tf_op jit(solution)/shard_map/ppermute | solution.py:66
  90.9 0.7 collective-permute-start.13
  91.6 0.7 collective-permute-start.14
  92.2 0.0 collective-permute-done.10.second
  92.3 0.1 collective-permute-start.15
  92.3 1.7 %shard_map.37.own_0 = f32[1,768]{1,0:T(1,128)S(1)} custom-call(s32[1]{0:T(128)} %bitcast.index_ref, bf16[784,1024]{1,0:T(8,128)(2,1)S(1)} %copy-done), custom_call_target="tpu_custom_call" | custom-call | flops 1207959552 | bytes 1572864 | tf_op jit(solution)/shard_map/pallas_call | solution.py:432
  94.0 0.0 collective-permute-done.11.first
  94.0 0.0 collective-permute-done.12.row
  94.0 0.0 collective-permute-done.13.top
  94.0 0.0 collective-permute-done.14.side
  94.1 1.9 %collective-permute-done.15.swap = f32[1,768]{1,0:T(1,128)S(1)} collective-permute-done((f32[1,768]{1,0:T(1,128)S(1)}, f32[1,768]{1,0:T(1,128)S(1)}, u32[]{:S(2)}, u32[]{:S(2)}) %collective-permute-start.15) | collective-permute-done | bytes 3104 | tf_op jit(solution)/shard_map/ppermute | solution.py:66
  95.9 0.6 finish.1
  (4 shorter events, 0.0 us)
Async XLA Ops:
  4.0 22.9 %collective-permute-start = (bf16[784,1024]{1,0:T(8,128)(2,1)}, bf16[784,1024]{1,0:T(8,128)(2,1)S(1)}, u32[]{:S(2)}, u32[]{:S(2)}) collective-permute-start(bf16[784,1024]{1,0:T(8,128)(2,1)} %pack.1.own_hbm), channel_id=1, source_target_pairs={{2,0},{3,1},{4,2},{5,3},{6,4},{7,5},{18,16},{19,17},{20,18},{21,19... | collective-permute-start | bytes 4816904 | tf_op jit(solution)/shard_map/ppermute | solution.py:66
  6.3 28.3 %collective-permute-start.3 = (bf16[784,1024]{1,0:T(8,128)(2,1)}, bf16[784,1024]{1,0:T(8,128)(2,1)S(1)}, u32[]{:S(2)}, u32[]{:S(2)}) collective-permute-start(bf16[784,1024]{1,0:T(8,128)(2,1)} %pack.1.own_hbm), channel_id=1, source_target_pairs={{8,9},{9,8},{10,11},{11,10},{12,13},{13,12},{14,15},{15,14},{24,25... | collective-permute-start | bytes 4816904 | tf_op jit(solution)/shard_map/ppermute | solution.py:66
  26.8 22.8 %collective-permute-start.1 = (bf16[784,1024]{1,0:T(8,128)(2,1)S(1)}, bf16[784,1024]{1,0:T(8,128)(2,1)}, u32[]{:S(2)}, u32[]{:S(2)}) collective-permute-start(bf16[784,1024]{1,0:T(8,128)(2,1)S(1)} %collective-permute-done.r1_hbm), channel_id=1, source_target_pairs={{2,0},{3,1},{4,2},{5,3},{18,16},{19,17},{20,18},{21,19},{10,12},{1... | collective-permute-start | bytes 4816904 | tf_op jit(solution)/shard_map/ppermute | solution.py:66
  29.2 1.2 %copy-start.1 = (bf16[784,1024]{1,0:T(8,128)(2,1)}, bf16[784,1024]{1,0:T(8,128)(2,1)S(1)}, u32[]{:S(2)}) copy-start(bf16[784,1024]{1,0:T(8,128)(2,1)S(1)} %collective-permute-done.r1_hbm) | copy-start | bytes 4816900
  30.4 21.8 %collective-permute-start.6 = (bf16[784,1024]{1,0:T(8,128)(2,1)}, bf16[784,1024]{1,0:T(8,128)(2,1)}, u32[]{:S(2)}, u32[]{:S(2)}) collective-permute-start(bf16[784,1024]{1,0:T(8,128)(2,1)} %pack.1.own_hbm), channel_id=1, source_target_pairs={{14,22},{15,23},{16,8},{17,9}} | collective-permute-start | bytes 4816904 | tf_op jit(solution)/shard_map/ppermute | solution.py:66
  32.2 31.2 %collective-permute-start.2 = (bf16[784,1024]{1,0:T(8,128)(2,1)}, bf16[784,1024]{1,0:T(8,128)(2,1)}, u32[]{:S(2)}, u32[]{:S(2)}) collective-permute-start(bf16[784,1024]{1,0:T(8,128)(2,1)} %pack.1.own_hbm), channel_id=1, source_target_pairs={{0,1},{1,0},{2,3},{3,2},{4,5},{5,4},{6,7},{7,6},{16,17},{17,16},{1... | collective-permute-start | bytes 4816904 | tf_op jit(solution)/shard_map/ppermute | solution.py:66
  34.6 36.8 %collective-permute-start.5 = (bf16[784,1024]{1,0:T(8,128)(2,1)S(1)}, bf16[784,1024]{1,0:T(8,128)(2,1)}, u32[]{:S(2)}, u32[]{:S(2)}) collective-permute-start(bf16[784,1024]{1,0:T(8,128)(2,1)S(1)} %collective-permute-done.3.odd_hbm), channel_id=1, source_target_pairs={{8,10},{9,11},{24,26},{25,27},{14,12},{15,13}} | collective-permute-start | bytes 4816904 | tf_op jit(solution)/shard_map/ppermute | solution.py:66
  49.6 24.3 %collective-permute-start.4 = (bf16[784,1024]{1,0:T(8,128)(2,1)}, bf16[784,1024]{1,0:T(8,128)(2,1)}, u32[]{:S(2)}, u32[]{:S(2)}) collective-permute-start(bf16[784,1024]{1,0:T(8,128)(2,1)} %collective-permute-done.1.r2_hbm), channel_id=1, source_target_pairs={{0,8},{1,9},{16,24},{17,25},{2,10},{3,11},{18,26},{19,27}} | collective-permute-start | bytes 4816904 | tf_op jit(solution)/shard_map/ppermute | solution.py:66
  52.1 24.4 %collective-permute-start.9 = (bf16[784,1024]{1,0:T(8,128)(2,1)}, bf16[784,1024]{1,0:T(8,128)(2,1)}, u32[]{:S(2)}, u32[]{:S(2)}) collective-permute-start(bf16[784,1024]{1,0:T(8,128)(2,1)} %collective-permute-done.6), channel_id=1, source_target_pairs={{22,12},{23,13}} | collective-permute-start | bytes 4816904 | tf_op jit(solution)/shard_map/ppermute | solution.py:66
  54.0 3.4 %copy-start = (bf16[784,1024]{1,0:T(8,128)(2,1)S(1)}, bf16[784,1024]{1,0:T(8,128)(2,1)}, u32[]{:S(2)}) copy-start(bf16[784,1024]{1,0:T(8,128)(2,1)} %pack.1.own_hbm) | copy-start | bytes 4816900
  57.4 1.4 %copy-start.2 = (bf16[784,1024]{1,0:T(8,128)(2,1)S(1)}, bf16[784,1024]{1,0:T(8,128)(2,1)}, u32[]{:S(2)}) copy-start(bf16[784,1024]{1,0:T(8,128)(2,1)} %copy-done.1) | copy-start | bytes 4816900
  58.8 2.0 %copy-start.3 = (bf16[784,1024]{1,0:T(8,128)(2,1)S(1)}, bf16[784,1024]{1,0:T(8,128)(2,1)}, u32[]{:S(2)}) copy-start(bf16[784,1024]{1,0:T(8,128)(2,1)} %copy-done.1) | copy-start | bytes 4816900
  60.9 1.1 %copy-start.4 = (bf16[400,1024]{1,0:T(8,128)(2,1)S(1)}, bf16[400,1024]{1,0:T(8,128)(2,1)}, u32[]{:S(2)}) copy-start(bf16[400,1024]{1,0:T(8,128)(2,1)} %slice.8) | copy-start | bytes 2457604
  62.0 23.7 %collective-permute-start.7 = (bf16[400,1024]{1,0:T(8,128)(2,1)S(1)}, bf16[400,1024]{1,0:T(8,128)(2,1)S(1)}, u32[]{:S(2)}, u32[]{:S(2)}) collective-permute-start(bf16[400,1024]{1,0:T(8,128)(2,1)S(1)} %copy-done.4), channel_id=1, source_target_pairs={{16,12},{17,13},{14,18},{15,19}} | collective-permute-start | bytes 2457608 | tf_op jit(solution)/shard_map/ppermute | solution.py:66
  63.3 22.4 %collective-permute-start.8 = (bf16[384,1024]{1,0:T(8,128)(2,1)S(1)}, bf16[384,1024]{1,0:T(8,128)(2,1)S(1)}, u32[]{:S(2)}, u32[]{:S(2)}) collective-permute-start(bf16[384,1024]{1,0:T(8,128)(2,1)S(1)} %slice.9), channel_id=1, source_target_pairs={{8,12},{9,13},{22,18},{23,19}} | collective-permute-start | bytes 2359304 | tf_op jit(solution)/shard_map/ppermute | solution.py:66
  71.4 20.8 %collective-permute-start.10 = (f32[1,768]{1,0:T(1,128)S(1)}, f32[1,768]{1,0:T(1,128)S(1)}, u32[]{:S(2)}, u32[]{:S(2)}) collective-permute-start(f32[1,768]{1,0:T(1,128)S(1)} %get-tuple-element.43), channel_id=1, source_target_pairs={{0,4},{1,5},{2,6},{3,7},{16,20},{17,21},{18,22},{19,23},{12,8},{13... | collective-permute-start | bytes 9224 | tf_op jit(solution)/shard_map/ppermute | solution.py:66
  73.9 20.1 %collective-permute-start.11 = (f32[1,768]{1,0:T(1,128)S(1)}, f32[1,768]{1,0:T(1,128)S(1)}, u32[]{:S(2)}, u32[]{:S(2)}) collective-permute-start(f32[1,768]{1,0:T(1,128)S(1)} %get-tuple-element.44), channel_id=1, source_target_pairs={{0,2},{1,3},{2,4},{3,5},{4,6},{5,7},{16,18},{17,19},{18,20},{19,21... | collective-permute-start | bytes 9224 | tf_op jit(solution)/shard_map/ppermute | solution.py:66
  89.6 4.4 %collective-permute-start.12 = (f32[1,768]{1,0:T(1,128)S(1)}, f32[1,768]{1,0:T(1,128)S(1)}, u32[]{:S(2)}, u32[]{:S(2)}) collective-permute-start(f32[1,768]{1,0:T(1,128)S(1)} %get-tuple-element.45), channel_id=1, source_target_pairs={{8,4},{9,5},{24,20},{25,21},{10,6},{11,7},{26,22},{27,23},{12,16},... | collective-permute-start | bytes 9224 | tf_op jit(solution)/shard_map/ppermute | solution.py:66
  90.9 3.1 %collective-permute-start.13 = (f32[1,768]{1,0:T(1,128)S(1)}, f32[1,768]{1,0:T(1,128)S(1)}, u32[]{:S(2)}, u32[]{:S(2)}) collective-permute-start(f32[1,768]{1,0:T(1,128)S(1)} %get-tuple-element.46), channel_id=1, source_target_pairs={{10,8},{11,9},{26,24},{27,25},{12,14},{13,15}} | collective-permute-start | bytes 9224 | tf_op jit(solution)/shard_map/ppermute | solution.py:66
  91.6 2.5 %collective-permute-start.14 = (f32[1,768]{1,0:T(1,128)S(1)}, f32[1,768]{1,0:T(1,128)S(1)}, u32[]{:S(2)}, u32[]{:S(2)}) collective-permute-start(f32[1,768]{1,0:T(1,128)S(1)} %get-tuple-element.47), channel_id=1, source_target_pairs={{10,9},{11,8},{26,25},{27,24},{12,15},{13,14}} | collective-permute-start | bytes 9224 | tf_op jit(solution)/shard_map/ppermute | solution.py:66
  92.3 3.7 %collective-permute-start.15 = (f32[1,768]{1,0:T(1,128)S(1)}, f32[1,768]{1,0:T(1,128)S(1)}, u32[]{:S(2)}, u32[]{:S(2)}) collective-permute-start(f32[1,768]{1,0:T(1,128)S(1)} %get-tuple-element.48), channel_id=1, source_target_pairs={{0,1},{1,0},{2,3},{3,2},{4,5},{5,4},{6,7},{7,6},{16,17},{17,16},{1... | collective-permute-start | bytes 9224 | tf_op jit(solution)/shard_map/ppermute | solution.py:66
